TPU v7x, 256 devices: a whole 4x4x8 slice. The times are simulated.
256 devices in a mesh: row: 8 (over y, core), col: 8 (over x, z_hi), rep: 4 (over z_lo).
Axes of the slice: x: 4, y: 4, z: 8 (z_hi: 2, z_lo: 4; z = z_hi * 4 + z_lo), core: 2. Of those that a mesh axis runs over, the one named last changes fastest.
Arguments:
- features: float32 [256, 32768], P('rep', ('col', 'row')), may hold values from -6 to 6
- weight: float32 [256, 256], replicated, may hold values from -0.375 to 0.375
- cotangent: float32 [256, 32768], P('rep', ('row', 'col')), may hold values from -6 to 6
- tile_values: float32 [10240, 128, 128], P(('row', 'col')), may hold values from -0.078125 to 0.078125
- tile_row: int32 [10240], P(('row', 'col')), may hold values from 0 to 31
- tile_col: int32 [10240], P(('row', 'col')), may hold values from 0 to 31
- tile_kind: int32 [10240], P(('row', 'col')), may hold values from 0 to 159
- tile_count: int32 [64], P(('row', 'col')), may hold values from 40 to 160, as said below
Outputs:
- output: float32 [256, 32768], P('rep', ('row', 'col'))
- input_grad: float32 [256, 32768], P('rep', ('col', 'row'))
- weight_grad: float32 [256, 256], P('rep')
Inputs may be any that keep to these rules, and one draw needn't show every extreme that they name: `tile_count`: a block's slots at or after its count are not part of the adjacency; some block uses all 160 slots. `tile_row`: slots may repeat a tile position; their tiles add. `tile_kind`: an index into the 160 stored tiles of the same block.
All inputs are finite; a program needn't handle non-finite values.
Results may differ from a plain program's by a relative error of at most 0.0001.
Values sent between devices are 32-bit elements; how exact they have to be, the bound alone decides.
No kernel may reach another device: no remote copies, remote signals or barrier semaphores. Data moves between devices by JAX's collectives and lax.ppermute only.
A program may use at most 128 MiB of HBM per device.

v0:
```python
import functools

import jax
import jax.numpy as jnp
from jax import lax
from jax.experimental import pallas as pl
from jax.experimental.pallas import tpu as pltpu
from jax.sharding import PartitionSpec as P


BF16 = jnp.bfloat16
F32 = jnp.float32
NT = (((1,), (1,)), ((), ()))
NN = (((1,), (0,)), ((), ()))
GROUP = 16
RING = 4
ROOT_2_PI = 0.7978845608028654
CUBIC = 0.044715

dot = functools.partial(lax.dot_general, preferred_element_type=F32)


def split(x):
    high = x.astype(BF16)
    return high, (x - high.astype(F32)).astype(BF16)


def dot3(a, b, dims):
    a_high, a_low = split(a)
    b_high, b_low = split(b)
    return dot(a_high, b_high, dims) + dot(a_high, b_low, dims) + dot(a_low, b_high, dims)


def spmm_kernel(transposed, n_in, n_out, table, *refs):
    sources = refs[:n_in]
    values = refs[n_in]
    outs = refs[n_in + 1 : n_in + 1 + n_out]
    buf, sem, held, acc = refs[n_in + 1 + n_out :]
    width, length = sources[0].shape
    edge = values.shape[-1]
    per = length // edge
    to_row, from_row = (2, 3) if transposed else (0, 1)
    groups = (table[5, 0] + GROUP - 1) // GROUP

    def copy(group, u):
        slot = lax.rem(group, RING)
        return pltpu.make_async_copy(
            values.at[table[4, group * GROUP + u]], buf.at[slot, u], sem.at[slot, u]
        )

    def start(group):
        def one(u, carry):
            copy(group, u).start()
            return carry

        lax.fori_loop(0, GROUP, one, 0, unroll=4)

    for g in range(RING - 1):

        @pl.when(g < groups)
        def _():
            start(g)

    for b in range(n_in):
        for j in range(per):
            high, low = split(sources[b][:, j * edge : (j + 1) * edge])
            held[b * per + j, :width] = high
            held[b * per + j, width:] = low
    acc[...] = jnp.zeros_like(acc)

    def step(group, carry):
        @pl.when(group + RING - 1 < groups)
        def _():
            start(group + RING - 1)

        for u in range(GROUP):
            copy(group, u).wait()
        slot = lax.rem(group, RING)
        products = []
        for u in range(GROUP):
            both = held[table[from_row, group * GROUP + u]]
            high, low = split(buf[slot, u])
            if transposed:
                p = dot(both, high, NN)
                products.append(p[:width] + p[width:] + dot(both[:width], low, NN))
            else:
                p = dot(both, jnp.concatenate([high, low], 0), NT)
                products.append(p[:width, :edge] + p[:width, edge:] + p[width:, :edge])
        for u in range(GROUP):
            to = table[to_row, group * GROUP + u]
            acc[to] = acc[to] + products[u]
        return carry

    lax.fori_loop(0, groups, step, 0)
    for b in range(n_out):
        for j in range(per):
            outs[b][:, j * edge : (j + 1) * edge] = acc[b * per + j]


def spmm(table, sources, values, n_out, transposed):
    n_in = len(sources)
    width, length = sources[0].shape
    slots, edge, _ = values.shape
    per = length // edge
    vmem = pl.BlockSpec(memory_space=pltpu.VMEM)
    return pl.pallas_call(
        functools.partial(spmm_kernel, transposed, n_in, n_out),
        in_specs=[pl.BlockSpec(memory_space=pltpu.SMEM)]
        + [vmem] * n_in
        + [pl.BlockSpec(memory_space=pl.ANY)],
        out_specs=[vmem] * n_out,
        out_shape=[jax.ShapeDtypeStruct((width, length), F32)] * n_out,
        scratch_shapes=[
            pltpu.VMEM((RING, GROUP, edge, edge), F32),
            pltpu.SemaphoreType.DMA((RING, GROUP)),
            pltpu.VMEM((n_in * per, 2 * width, edge), BF16),
            pltpu.VMEM((n_out * per + 1, width, edge), F32),
        ],
        compiler_params=pltpu.CompilerParams(vmem_limit_bytes=51 << 20),
        cost_estimate=pl.CostEstimate(
            flops=6 * slots * width * edge * edge, bytes_accessed=14 << 20, transcendentals=0
        ),
        name="spmm_back" if transposed else "spmm",
    )(table, *sources, values)


def mid_kernel(n_rep, place, *refs):
    aggs = refs[:n_rep]
    cots = refs[n_rep : 2 * n_rep]
    weight, weight_t, out, mixed_grad, grad_pre = refs[2 * n_rep : 2 * n_rep + 5]
    agg, cot, act = refs[2 * n_rep + 5 :]
    quarter = aggs[0].shape[0]
    me = place[0]
    for k in range(n_rep):
        at = pl.ds(pl.multiple_of((me ^ k) * quarter, quarter), quarter)
        agg[at, :] = aggs[k][...]
        cot[at, :] = cots[k][...]
    pre = dot3(weight_t[...], agg[...], NN)
    square = pre * pre
    curve = jnp.tanh(ROOT_2_PI * (pre + CUBIC * (square * pre)))
    half = 0.5 * (1.0 + curve)
    act[...] = pre * half
    slope = half + 0.5 * pre * (1.0 - curve * curve) * (
        ROOT_2_PI * (1.0 + 3.0 * CUBIC * square)
    )
    grad = cot[...] * slope
    grad_pre[...] = grad
    own = pl.ds(pl.multiple_of(me * quarter, quarter), quarter)
    mixed_grad[...] = dot3(weight[own, :], grad, NN)
    out[...] = act[own, :]


def mid(place, aggs, cots, weight, weight_t):
    n_rep = len(aggs)
    quarter, length = aggs[0].shape
    width = weight.shape[0]
    vmem = pl.BlockSpec(memory_space=pltpu.VMEM)
    return pl.pallas_call(
        functools.partial(mid_kernel, n_rep),
        in_specs=[pl.BlockSpec(memory_space=pltpu.SMEM)] + [vmem] * (2 * n_rep + 2),
        out_specs=[vmem] * 3,
        out_shape=[
            jax.ShapeDtypeStruct((quarter, length), F32),
            jax.ShapeDtypeStruct((quarter, length), F32),
            jax.ShapeDtypeStruct((width, length), F32),
        ],
        scratch_shapes=[pltpu.VMEM((width, length), F32)] * 3,
        compiler_params=pltpu.CompilerParams(vmem_limit_bytes=16 << 20),
        cost_estimate=pl.CostEstimate(
            flops=8 * width * width * length, bytes_accessed=4 << 20, transcendentals=0
        ),
        name="mid",
    )(place, *aggs, *cots, weight, weight_t)


def weight_kernel(scale, agg, grad_pre, out):
    out[...] = dot3(agg[...], grad_pre[...], NT) * scale


def weight_part(agg, grad_pre, scale):
    vmem = pl.BlockSpec(memory_space=pltpu.VMEM)
    return pl.pallas_call(
        functools.partial(weight_kernel, scale),
        in_specs=[vmem, vmem],
        out_specs=vmem,
        out_shape=jax.ShapeDtypeStruct((agg.shape[0], grad_pre.shape[0]), F32),
        compiler_params=pltpu.CompilerParams(vmem_limit_bytes=16 << 20),
        cost_estimate=pl.CostEstimate(
            flops=6 * agg.shape[0] * grad_pre.size, bytes_accessed=1 << 20, transcendentals=0
        ),
        name="weight_part",
    )(agg, grad_pre)


def shift(x, axis, by):
    n = lax.axis_size(axis)
    return lax.ppermute(x, axis, [(i, (i + by) % n) for i in range(n)])


def swap(x, axis, bit):
    n = lax.axis_size(axis)
    return lax.ppermute(x, axis, [(i, i ^ bit) for i in range(n)])


def layer(features, weight, cotangent, tile_values, tile_row, tile_col, tile_kind, tile_count):
    n_row, n_col, n_rep = (lax.axis_size(a) for a in ("row", "col", "rep"))
    row, col, rep = (lax.axis_index(a) for a in ("row", "col", "rep"))
    stretch = features.shape[1]
    per = stretch // tile_values.shape[1]
    slots = tile_kind.shape[0]

    def relative(tile, at, n):
        stretch_of = tile // per
        far = (stretch_of // 2 - at // 2) % (n // 2)
        return (far * 2 + ((stretch_of ^ at) & 1)) * per + tile % per

    live = jnp.arange(slots, dtype=jnp.int32) < tile_count[0]
    by_row = relative(tile_row, col, n_col)
    by_col = relative(tile_col, row, n_row)
    table = jnp.stack(
        [
            jnp.where(live, by_row, n_col * per),
            by_col,
            jnp.where(live, by_col, n_row * per),
            by_row,
            tile_kind,
            jnp.broadcast_to(tile_count, (slots,)),
        ]
    )
    blocks = []
    for k in range(n_row // 2):
        mine = features if k == 0 else shift(features, "row", -2 * k)
        blocks += [mine, swap(mine, "row", 1)]
    cots = [cotangent] + [swap(cotangent, "rep", k) for k in range(1, n_rep)]
    table, *cots[1:] = lax.optimization_barrier((table, *cots[1:]))
    parts = spmm(table, blocks, tile_values, n_col, False)
    sums = [None, None]
    for z in (1, 0):
        total = parts[z]
        for k in range(1, n_col // 2):
            total = total + shift(parts[2 * k + z], "col", 2 * k)
        sums[z] = total
    agg = sums[0] + swap(sums[1], "col", 1)
    aggs = [agg] + [swap(agg, "rep", k) for k in range(1, n_rep)]
    place = rep.astype(jnp.int32)[None]
    output, mixed_grad, grad_pre = mid(place, aggs, cots, weight, weight.T)
    far = swap(mixed_grad, "col", 1)
    blocks = [mixed_grad, far]
    for k in range(1, n_col // 2):
        blocks += [shift(mixed_grad, "col", -2 * k), shift(far, "col", -2 * k)]
    node_total = stretch * n_row * n_col
    weight_grad = weight_part(agg, grad_pre, float(node_total) ** (-0.5))

    def add_swapped(x, axis, bit):
        return x + swap(x, axis, bit)

    weight_grad = add_swapped(weight_grad, "row", 1)
    weight_grad = add_swapped(weight_grad, "row", 2)
    weight_grad = add_swapped(weight_grad, "row", 4)
    weight_grad = add_swapped(weight_grad, "col", 1)
    parts = spmm(table, blocks, tile_values, n_row, True)
    totals = [parts[2 * k] + swap(parts[2 * k + 1], "row", 1) for k in range(n_row // 2)]
    input_grad = totals[0]
    for k in (2, 1, 3):
        got = shift(totals[k], "row", 2 * k)
        input_grad = input_grad + got
    weight_grad = add_swapped(weight_grad, "col", 2)
    weight_grad = add_swapped(weight_grad, "col", 4)
    return (output, input_grad, weight_grad)


def solution(mesh):
    return jax.shard_map(
        layer,
        mesh=mesh,
        in_specs=(
            P("rep", ("col", "row")),
            P(),
            P("rep", ("row", "col")),
            P(("row", "col"), None, None),
            P(("row", "col")),
            P(("row", "col")),
            P(("row", "col")),
            P(("row", "col")),
        ),
        out_specs=(P("rep", ("row", "col")), P("rep", ("col", "row")), P("rep", None)),
        check_vma=False,
    )
```

profile of v0, /device:TPU:2, one launch (start us, length us, event | category | flops | bytes accessed | tf_op | source)
XLA Modules:
  0.0 116.8 jit_solution(6078847191118982095)
XLA Ops:
  0.6 3.4 %collective-permute-start.1 = (f32[64,512]{1,0:T(8,128)}, f32[64,512]{1,0:T(8,128)S(1)}, u32[]{:S(2)}, u32[]{:S(2)}) collective-permute-start(f32[64,512]{1,0:T(8,128)} %refs_4_.1), channel_id=1, source_target_pairs={{0,2},{1,3},{2,0},{3,1},{4,6},{5,7},{6,4},{7,5},{8,10},{9,11},{10,... | collective-permute-start | bytes 393224 | tf_op jit(solution)/shard_map/ppermute | solution.py:202
  4.0 1.9 %collective-permute-start = (f32[64,512]{1,0:T(8,128)}, f32[64,512]{1,0:T(8,128)S(1)}, u32[]{:S(2)}, u32[]{:S(2)}) collective-permute-start(f32[64,512]{1,0:T(8,128)} %refs_4_.1), channel_id=1, source_target_pairs={{0,1},{1,0},{2,3},{3,2},{4,5},{5,4},{6,7},{7,6},{8,9},{9,8},{10,11... | collective-permute-start | bytes 393224 | tf_op jit(solution)/shard_map/ppermute | solution.py:202
  5.9 3.2 %collective-permute-start.6 = (f32[64,512]{1,0:T(8,128)}, f32[64,512]{1,0:T(8,128)S(1)}, u32[]{:S(2)}, u32[]{:S(2)}) collective-permute-start(f32[64,512]{1,0:T(8,128)} %refs_0_.1), channel_id=1, source_target_pairs={{0,128},{32,160},{64,192},{96,224},{128,0},{160,32},{192,64},{224,... | collective-permute-start | bytes 393224 | tf_op jit(solution)/shard_map/ppermute | solution.py:197
  11.8 2.2 %collective-permute-start.2 = (f32[64,512]{1,0:T(8,128)}, f32[64,512]{1,0:T(8,128)S(1)}, u32[]{:S(2)}, u32[]{:S(2)}) collective-permute-start(f32[64,512]{1,0:T(8,128)} %refs_4_.1), channel_id=1, source_target_pairs={{0,3},{1,2},{2,1},{3,0},{4,7},{5,6},{6,5},{7,4},{8,11},{9,10},{10,... | collective-permute-start | bytes 393224 | tf_op jit(solution)/shard_map/ppermute | solution.py:202
  19.9 5.7 %spmm.1 = (f32[64,512]{1,0:T(8,128)S(1)}, f32[64,512]{1,0:T(8,128)S(1)}, f32[64,512]{1,0:T(8,128)S(1)}, f32[64,512]{1,0:T(8,128)S(1)}, f32[64,512]{1,0:T(8,128)S...) custom-call(s32[6,160]{1,0:T(8,128)S(1)} %stack.23.table, f32[64,512]{1,0:T(8,128)S(1)} %copy-done.1, ...), custom_call_target="tpu_custom_call" | custom-call | flops 1006632960 | bytes 14680064 | tf_op jit(solution)/shard_map/spmm/pallas_call | solution.py:106
  25.6 2.7 %collective-permute-start.13 = (f32[64,512]{1,0:T(8,128)S(1)}, f32[64,512]{1,0:T(8,128)S(1)}, u32[]{:S(2)}, u32[]{:S(2)}) collective-permute-start(f32[64,512]{1,0:T(8,128)S(1)} %get-tuple-element.32), channel_id=1, source_target_pairs={{0,8},{4,12},{8,16},{12,20},{16,24},{20,28},{24,0},{28,4},{1,9},{5... | collective-permute-start | bytes 393224 | tf_op jit(solution)/shard_map/ppermute | solution.py:197
  28.3 2.3 %collective-permute-start.14 = (f32[64,512]{1,0:T(8,128)S(1)}, f32[64,512]{1,0:T(8,128)S(1)}, u32[]{:S(2)}, u32[]{:S(2)}) collective-permute-start(f32[64,512]{1,0:T(8,128)S(1)} %get-tuple-element.33), channel_id=1, source_target_pairs={{0,16},{4,20},{8,24},{12,28},{16,0},{20,4},{24,8},{28,12},{1,17},{... | collective-permute-start | bytes 393224 | tf_op jit(solution)/shard_map/ppermute | solution.py:197
  30.6 2.0 %collective-permute-start.10 = (f32[64,512]{1,0:T(8,128)S(1)}, f32[64,512]{1,0:T(8,128)S(1)}, u32[]{:S(2)}, u32[]{:S(2)}) collective-permute-start(f32[64,512]{1,0:T(8,128)S(1)} %get-tuple-element.28), channel_id=1, source_target_pairs={{0,8},{4,12},{8,16},{12,20},{16,24},{20,28},{24,0},{28,4},{1,9},{5... | collective-permute-start | bytes 393224 | tf_op jit(solution)/shard_map/ppermute | solution.py:197
  32.7 2.4 %collective-permute-start.11 = (f32[64,512]{1,0:T(8,128)S(1)}, f32[64,512]{1,0:T(8,128)S(1)}, u32[]{:S(2)}, u32[]{:S(2)}) collective-permute-start(f32[64,512]{1,0:T(8,128)S(1)} %get-tuple-element.29), channel_id=1, source_target_pairs={{0,16},{4,20},{8,24},{12,28},{16,0},{20,4},{24,8},{28,12},{1,17},{... | collective-permute-start | bytes 393224 | tf_op jit(solution)/shard_map/ppermute | solution.py:197
  35.1 3.8 %collective-permute-start.12 = (f32[64,512]{1,0:T(8,128)S(1)}, f32[64,512]{1,0:T(8,128)S(1)}, u32[]{:S(2)}, u32[]{:S(2)}) collective-permute-start(f32[64,512]{1,0:T(8,128)S(1)} %get-tuple-element.30), channel_id=1, source_target_pairs={{0,24},{4,28},{8,0},{12,4},{16,8},{20,12},{24,16},{28,20},{1,25},{... | collective-permute-start | bytes 393224 | tf_op jit(solution)/shard_map/ppermute | solution.py:197
  38.9 1.9 %collective-permute-done.15 = f32[64,512]{1,0:T(8,128)S(1)} collective-permute-done((f32[64,512]{1,0:T(8,128)S(1)}, f32[64,512]{1,0:T(8,128)S(1)}, u32[]{:S(2)}, u32[]{:S(2)}) %collective-permute-start.15) | collective-permute-done | bytes 131104 | tf_op jit(solution)/shard_map/ppermute | solution.py:197
  40.8 3.6 %collective-permute-start.16 = (f32[64,512]{1,0:T(8,128)S(1)}, f32[64,512]{1,0:T(8,128)S(1)}, u32[]{:S(2)}, u32[]{:S(2)}) collective-permute-start(f32[64,512]{1,0:T(8,128)S(1)} %add_add_fusion.1), channel_id=1, source_target_pairs={{0,4},{4,0},{8,12},{12,8},{16,20},{20,16},{24,28},{28,24},{1,5},{5... | collective-permute-start | bytes 393224 | tf_op jit(solution)/shard_map/ppermute | solution.py:202
  44.4 5.4 %collective-permute-done.16 = f32[64,512]{1,0:T(8,128)S(1)} collective-permute-done((f32[64,512]{1,0:T(8,128)S(1)}, f32[64,512]{1,0:T(8,128)S(1)}, u32[]{:S(2)}, u32[]{:S(2)}) %collective-permute-start.16) | collective-permute-done | bytes 131104 | tf_op jit(solution)/shard_map/ppermute | solution.py:202
  49.9 2.2 %collective-permute-start.19 = (f32[64,512]{1,0:T(8,128)S(1)}, f32[64,512]{1,0:T(8,128)S(1)}, u32[]{:S(2)}, u32[]{:S(2)}) collective-permute-start(f32[64,512]{1,0:T(8,128)S(1)} %add_add_fusion.2.refs_0_.agg), channel_id=1, source_target_pairs={{0,3},{1,2},{2,1},{3,0},{4,7},{5,6},{6,5},{7,4},{8,11},{9,10},{10,... | collective-permute-start | bytes 393224 | tf_op jit(solution)/shard_map/ppermute | solution.py:202
  52.1 2.4 %collective-permute-start.17 = (f32[64,512]{1,0:T(8,128)S(1)}, f32[64,512]{1,0:T(8,128)S(1)}, u32[]{:S(2)}, u32[]{:S(2)}) collective-permute-start(f32[64,512]{1,0:T(8,128)S(1)} %add_add_fusion.2.refs_0_.agg), channel_id=1, source_target_pairs={{0,1},{1,0},{2,3},{3,2},{4,5},{5,4},{6,7},{7,6},{8,9},{9,8},{10,11... | collective-permute-start | bytes 393224 | tf_op jit(solution)/shard_map/ppermute | solution.py:202
  54.6 2.4 %collective-permute-done.19.refs_3_ = f32[64,512]{1,0:T(8,128)S(1)} collective-permute-done((f32[64,512]{1,0:T(8,128)S(1)}, f32[64,512]{1,0:T(8,128)S(1)}, u32[]{:S(2)}, u32[]{:S(2)}) %collective-permute-start.19) | collective-permute-done | bytes 131104 | tf_op jit(solution)/shard_map/ppermute | solution.py:202
  57.1 3.4 %collective-permute-done.18.refs_2_ = f32[64,512]{1,0:T(8,128)S(1)} collective-permute-done((f32[64,512]{1,0:T(8,128)S(1)}, f32[64,512]{1,0:T(8,128)S(1)}, u32[]{:S(2)}, u32[]{:S(2)}) %collective-permute-start.18) | collective-permute-done | bytes 131104 | tf_op jit(solution)/shard_map/ppermute | solution.py:202
  60.5 1.4 %mid.1 = (f32[64,512]{1,0:T(8,128)}, f32[64,512]{1,0:T(8,128)S(1)}, f32[256,512]{1,0:T(8,128)S(1)}) custom-call(s32[1]{0:T(128)} %bitcast.place, f32[64,512]{1,0:T(8,128)S(1)} %add_add_fusion.2.refs_0_.agg, f32[64,512]{1,0:T(8,128)S(1)} %collective-permute-done.17.refs_1_, f32[64,512]{1,0:T(8,128)S(1)} %collective-permute-done.18.refs_2_, ...), custom_call_target="tpu_custom_call" | custom-call | flops 268435456 | bytes 4194304 | tf_op jit(solution)/shard_map/mid/pallas_call | solution.py:158
  62.4 5.3 %collective-permute-start.20 = (f32[64,512]{1,0:T(8,128)S(1)}, f32[64,512]{1,0:T(8,128)S(1)}, u32[]{:S(2)}, u32[]{:S(2)}) collective-permute-start(f32[64,512]{1,0:T(8,128)S(1)} %get-tuple-element.39.refs_0_), channel_id=1, source_target_pairs={{0,4},{4,0},{8,12},{12,8},{16,20},{20,16},{24,28},{28,24},{1,5},{5... | collective-permute-start | bytes 393224 | tf_op jit(solution)/shard_map/ppermute | solution.py:202
  70.1 2.6 %collective-permute-start.21 = (f32[64,512]{1,0:T(8,128)S(1)}, f32[64,512]{1,0:T(8,128)S(1)}, u32[]{:S(2)}, u32[]{:S(2)}) collective-permute-start(f32[64,512]{1,0:T(8,128)S(1)} %get-tuple-element.39.refs_0_), channel_id=1, source_target_pairs={{0,24},{4,28},{8,0},{12,4},{16,8},{20,12},{24,16},{28,20},{1,25},{... | collective-permute-start | bytes 393224 | tf_op jit(solution)/shard_map/ppermute | solution.py:197
  72.8 2.7 %collective-permute-start.26 = (f32[64,512]{1,0:T(8,128)S(1)}, f32[64,512]{1,0:T(8,128)S(1)}, u32[]{:S(2)}, u32[]{:S(2)}) collective-permute-start(f32[64,512]{1,0:T(8,128)S(1)} %collective-permute-done.20.refs_1_), channel_id=1, source_target_pairs={{0,8},{4,12},{8,16},{12,20},{16,24},{20,28},{24,0},{28,4},{1,9},{5... | collective-permute-start | bytes 393224 | tf_op jit(solution)/shard_map/ppermute | solution.py:197
  75.5 2.0 %collective-permute-start.24 = (f32[64,512]{1,0:T(8,128)S(1)}, f32[64,512]{1,0:T(8,128)S(1)}, u32[]{:S(2)}, u32[]{:S(2)}) collective-permute-start(f32[64,512]{1,0:T(8,128)S(1)} %collective-permute-done.20.refs_1_), channel_id=1, source_target_pairs={{0,16},{4,20},{8,24},{12,28},{16,0},{20,4},{24,8},{28,12},{1,17},{... | collective-permute-start | bytes 393224 | tf_op jit(solution)/shard_map/ppermute | solution.py:197
  77.6 6.6 %collective-permute-start.36 = (f32[64,256]{1,0:T(8,128)S(1)}, f32[64,256]{1,0:T(8,128)S(1)}, u32[]{:S(2)}, u32[]{:S(2)}) collective-permute-start(f32[64,256]{1,0:T(8,128)S(1)} %add.119), channel_id=1, source_target_pairs={{0,128},{32,160},{64,192},{96,224},{128,0},{160,32},{192,64},{224,... | collective-permute-start | bytes 196616 | tf_op jit(solution)/shard_map/ppermute | solution.py:202
  84.4 5.7 %spmm_back.1 = (f32[64,512]{1,0:T(8,128)S(1)}, f32[64,512]{1,0:T(8,128)S(1)}, f32[64,512]{1,0:T(8,128)S(1)}, f32[64,512]{1,0:T(8,128)S(1)}, f32[64,512]{1,0:T(8,...) custom-call(s32[6,160]{1,0:T(8,128)S(1)} %stack.23.table, ...), custom_call_target="tpu_custom_call" | custom-call | flops 1006632960 | bytes 14680064 | tf_op jit(solution)/shard_map/spmm_back/pallas_call | solution.py:106
  90.9 4.9 %collective-permute-start.37 = (f32[64,256]{1,0:T(8,128)S(1)}, f32[64,256]{1,0:T(8,128)S(1)}, u32[]{:S(2)}, u32[]{:S(2)}) collective-permute-start(f32[64,256]{1,0:T(8,128)S(1)} %add.120), channel_id=1, source_target_pairs={{0,4},{4,0},{8,12},{12,8},{16,20},{20,16},{24,28},{28,24},{1,5},{5... | collective-permute-start | bytes 196616 | tf_op jit(solution)/shard_map/ppermute | solution.py:202
  95.8 3.6 %collective-permute-done.37 = f32[64,256]{1,0:T(8,128)S(1)} collective-permute-done((f32[64,256]{1,0:T(8,128)S(1)}, f32[64,256]{1,0:T(8,128)S(1)}, u32[]{:S(2)}, u32[]{:S(2)}) %collective-permute-start.37) | collective-permute-done | bytes 65568 | tf_op jit(solution)/shard_map/ppermute | solution.py:202
  99.4 3.0 %collective-permute-start.38 = (f32[64,256]{1,0:T(8,128)S(1)}, f32[64,256]{1,0:T(8,128)S(1)}, u32[]{:S(2)}, u32[]{:S(2)}) collective-permute-start(f32[64,256]{1,0:T(8,128)S(1)} %add.121), channel_id=1, source_target_pairs={{0,8},{4,12},{8,0},{12,4},{16,24},{20,28},{24,16},{28,20},{1,9},{5... | collective-permute-start | bytes 196616 | tf_op jit(solution)/shard_map/ppermute | solution.py:202
  102.4 3.6 %collective-permute-start.29 = (f32[64,512]{1,0:T(8,128)S(1)}, f32[64,512]{1,0:T(8,128)S(1)}, u32[]{:S(2)}, u32[]{:S(2)}) collective-permute-start(f32[64,512]{1,0:T(8,128)S(1)} %add.112), channel_id=1, source_target_pairs={{0,128},{32,160},{64,192},{96,224},{128,0},{160,32},{192,64},{224,... | collective-permute-start | bytes 393224 | tf_op jit(solution)/shard_map/ppermute | solution.py:197
  106.1 1.9 %collective-permute-start.31 = (f32[64,512]{1,0:T(8,128)S(1)}, f32[64,512]{1,0:T(8,128)S(1)}, u32[]{:S(2)}, u32[]{:S(2)}) collective-permute-start(f32[64,512]{1,0:T(8,128)S(1)} %add.114), channel_id=1, source_target_pairs={{0,64},{32,96},{64,128},{96,160},{128,192},{160,224},{192,0},{224,... | collective-permute-start | bytes 393224 | tf_op jit(solution)/shard_map/ppermute | solution.py:197
  108.0 1.5 %collective-permute-start.33 = (f32[64,512]{1,0:T(8,128)S(1)}, f32[64,512]{1,0:T(8,128)S(1)}, u32[]{:S(2)}, u32[]{:S(2)}) collective-permute-start(f32[64,512]{1,0:T(8,128)S(1)} %add.116), channel_id=1, source_target_pairs={{0,192},{32,224},{64,0},{96,32},{128,64},{160,96},{192,128},{224,1... | collective-permute-start | bytes 393224 | tf_op jit(solution)/shard_map/ppermute | solution.py:197
  109.5 2.9 %collective-permute-start.39 = (f32[64,256]{1,0:T(8,128)S(1)}, f32[64,256]{1,0:T(8,128)S(1)}, u32[]{:S(2)}, u32[]{:S(2)}) collective-permute-start(f32[64,256]{1,0:T(8,128)S(1)} %add.122), channel_id=1, source_target_pairs={{0,16},{4,20},{8,24},{12,28},{16,0},{20,4},{24,8},{28,12},{1,17},{... | collective-permute-start | bytes 196616 | tf_op jit(solution)/shard_map/ppermute | solution.py:202
  112.4 3.0 %collective-permute-done.39 = f32[64,256]{1,0:T(8,128)S(1)} collective-permute-done((f32[64,256]{1,0:T(8,128)S(1)}, f32[64,256]{1,0:T(8,128)S(1)}, u32[]{:S(2)}, u32[]{:S(2)}) %collective-permute-start.39) | collective-permute-done | bytes 65568 | tf_op jit(solution)/shard_map/ppermute | solution.py:202
  (74 shorter events, 13.5 us)
Async XLA Ops:
  0.6 11.2 %collective-permute-start.1 = (f32[64,512]{1,0:T(8,128)}, f32[64,512]{1,0:T(8,128)S(1)}, u32[]{:S(2)}, u32[]{:S(2)}) collective-permute-start(f32[64,512]{1,0:T(8,128)} %refs_4_.1), channel_id=1, source_target_pairs={{0,2},{1,3},{2,0},{3,1},{4,6},{5,7},{6,4},{7,5},{8,10},{9,11},{10,... | collective-permute-start | bytes 393224 | tf_op jit(solution)/shard_map/ppermute | solution.py:202
  4.0 10.1 %collective-permute-start = (f32[64,512]{1,0:T(8,128)}, f32[64,512]{1,0:T(8,128)S(1)}, u32[]{:S(2)}, u32[]{:S(2)}) collective-permute-start(f32[64,512]{1,0:T(8,128)} %refs_4_.1), channel_id=1, source_target_pairs={{0,1},{1,0},{2,3},{3,2},{4,5},{5,4},{6,7},{7,6},{8,9},{9,8},{10,11... | collective-permute-start | bytes 393224 | tf_op jit(solution)/shard_map/ppermute | solution.py:202
  5.9 8.1 %collective-permute-start.6 = (f32[64,512]{1,0:T(8,128)}, f32[64,512]{1,0:T(8,128)S(1)}, u32[]{:S(2)}, u32[]{:S(2)}) collective-permute-start(f32[64,512]{1,0:T(8,128)} %refs_0_.1), channel_id=1, source_target_pairs={{0,128},{32,160},{64,192},{96,224},{128,0},{160,32},{192,64},{224,... | collective-permute-start | bytes 393224 | tf_op jit(solution)/shard_map/ppermute | solution.py:197
  11.8 7.2 %collective-permute-start.2 = (f32[64,512]{1,0:T(8,128)}, f32[64,512]{1,0:T(8,128)S(1)}, u32[]{:S(2)}, u32[]{:S(2)}) collective-permute-start(f32[64,512]{1,0:T(8,128)} %refs_4_.1), channel_id=1, source_target_pairs={{0,3},{1,2},{2,1},{3,0},{4,7},{5,6},{6,5},{7,4},{8,11},{9,10},{10,... | collective-permute-start | bytes 393224 | tf_op jit(solution)/shard_map/ppermute | solution.py:202
  25.6 9.5 %collective-permute-start.13 = (f32[64,512]{1,0:T(8,128)S(1)}, f32[64,512]{1,0:T(8,128)S(1)}, u32[]{:S(2)}, u32[]{:S(2)}) collective-permute-start(f32[64,512]{1,0:T(8,128)S(1)} %get-tuple-element.32), channel_id=1, source_target_pairs={{0,8},{4,12},{8,16},{12,20},{16,24},{20,28},{24,0},{28,4},{1,9},{5... | collective-permute-start | bytes 393224 | tf_op jit(solution)/shard_map/ppermute | solution.py:197
  28.3 10.6 %collective-permute-start.14 = (f32[64,512]{1,0:T(8,128)S(1)}, f32[64,512]{1,0:T(8,128)S(1)}, u32[]{:S(2)}, u32[]{:S(2)}) collective-permute-start(f32[64,512]{1,0:T(8,128)S(1)} %get-tuple-element.33), channel_id=1, source_target_pairs={{0,16},{4,20},{8,24},{12,28},{16,0},{20,4},{24,8},{28,12},{1,17},{... | collective-permute-start | bytes 393224 | tf_op jit(solution)/shard_map/ppermute | solution.py:197
  30.6 10.1 %collective-permute-start.15 = (f32[64,512]{1,0:T(8,128)S(1)}, f32[64,512]{1,0:T(8,128)S(1)}, u32[]{:S(2)}, u32[]{:S(2)}) collective-permute-start(f32[64,512]{1,0:T(8,128)S(1)} %get-tuple-element.34), channel_id=1, source_target_pairs={{0,24},{4,28},{8,0},{12,4},{16,8},{20,12},{24,16},{28,20},{1,25},{... | collective-permute-start | bytes 393224 | tf_op jit(solution)/shard_map/ppermute | solution.py:197
  30.6 13.8 %collective-permute-start.10 = (f32[64,512]{1,0:T(8,128)S(1)}, f32[64,512]{1,0:T(8,128)S(1)}, u32[]{:S(2)}, u32[]{:S(2)}) collective-permute-start(f32[64,512]{1,0:T(8,128)S(1)} %get-tuple-element.28), channel_id=1, source_target_pairs={{0,8},{4,12},{8,16},{12,20},{16,24},{20,28},{24,0},{28,4},{1,9},{5... | collective-permute-start | bytes 393224 | tf_op jit(solution)/shard_map/ppermute | solution.py:197
  32.7 11.7 %collective-permute-start.11 = (f32[64,512]{1,0:T(8,128)S(1)}, f32[64,512]{1,0:T(8,128)S(1)}, u32[]{:S(2)}, u32[]{:S(2)}) collective-permute-start(f32[64,512]{1,0:T(8,128)S(1)} %get-tuple-element.29), channel_id=1, source_target_pairs={{0,16},{4,20},{8,24},{12,28},{16,0},{20,4},{24,8},{28,12},{1,17},{... | collective-permute-start | bytes 393224 | tf_op jit(solution)/shard_map/ppermute | solution.py:197
  35.1 9.3 %collective-permute-start.12 = (f32[64,512]{1,0:T(8,128)S(1)}, f32[64,512]{1,0:T(8,128)S(1)}, u32[]{:S(2)}, u32[]{:S(2)}) collective-permute-start(f32[64,512]{1,0:T(8,128)S(1)} %get-tuple-element.30), channel_id=1, source_target_pairs={{0,24},{4,28},{8,0},{12,4},{16,8},{20,12},{24,16},{28,20},{1,25},{... | collective-permute-start | bytes 393224 | tf_op jit(solution)/shard_map/ppermute | solution.py:197
  40.8 9.0 %collective-permute-start.16 = (f32[64,512]{1,0:T(8,128)S(1)}, f32[64,512]{1,0:T(8,128)S(1)}, u32[]{:S(2)}, u32[]{:S(2)}) collective-permute-start(f32[64,512]{1,0:T(8,128)S(1)} %add_add_fusion.1), channel_id=1, source_target_pairs={{0,4},{4,0},{8,12},{12,8},{16,20},{20,16},{24,28},{28,24},{1,5},{5... | collective-permute-start | bytes 393224 | tf_op jit(solution)/shard_map/ppermute | solution.py:202
  49.9 7.2 %collective-permute-start.19 = (f32[64,512]{1,0:T(8,128)S(1)}, f32[64,512]{1,0:T(8,128)S(1)}, u32[]{:S(2)}, u32[]{:S(2)}) collective-permute-start(f32[64,512]{1,0:T(8,128)S(1)} %add_add_fusion.2.refs_0_.agg), channel_id=1, source_target_pairs={{0,3},{1,2},{2,1},{3,0},{4,7},{5,6},{6,5},{7,4},{8,11},{9,10},{10,... | collective-permute-start | bytes 393224 | tf_op jit(solution)/shard_map/ppermute | solution.py:202
  52.1 8.4 %collective-permute-start.18 = (f32[64,512]{1,0:T(8,128)S(1)}, f32[64,512]{1,0:T(8,128)S(1)}, u32[]{:S(2)}, u32[]{:S(2)}) collective-permute-start(f32[64,512]{1,0:T(8,128)S(1)} %add_add_fusion.2.refs_0_.agg), channel_id=1, source_target_pairs={{0,2},{1,3},{2,0},{3,1},{4,6},{5,7},{6,4},{7,5},{8,10},{9,11},{10,... | collective-permute-start | bytes 393224 | tf_op jit(solution)/shard_map/ppermute | solution.py:202
  52.1 8.4 %collective-permute-start.17 = (f32[64,512]{1,0:T(8,128)S(1)}, f32[64,512]{1,0:T(8,128)S(1)}, u32[]{:S(2)}, u32[]{:S(2)}) collective-permute-start(f32[64,512]{1,0:T(8,128)S(1)} %add_add_fusion.2.refs_0_.agg), channel_id=1, source_target_pairs={{0,1},{1,0},{2,3},{3,2},{4,5},{5,4},{6,7},{7,6},{8,9},{9,8},{10,11... | collective-permute-start | bytes 393224 | tf_op jit(solution)/shard_map/ppermute | solution.py:202
  62.4 10.3 %collective-permute-start.20 = (f32[64,512]{1,0:T(8,128)S(1)}, f32[64,512]{1,0:T(8,128)S(1)}, u32[]{:S(2)}, u32[]{:S(2)}) collective-permute-start(f32[64,512]{1,0:T(8,128)S(1)} %get-tuple-element.39.refs_0_), channel_id=1, source_target_pairs={{0,4},{4,0},{8,12},{12,8},{16,20},{20,16},{24,28},{28,24},{1,5},{5... | collective-permute-start | bytes 393224 | tf_op jit(solution)/shard_map/ppermute | solution.py:202
  67.7 9.7 %collective-permute-start.25 = (f32[64,512]{1,0:T(8,128)S(1)}, f32[64,512]{1,0:T(8,128)S(1)}, u32[]{:S(2)}, u32[]{:S(2)}) collective-permute-start(f32[64,512]{1,0:T(8,128)S(1)} %get-tuple-element.39.refs_0_), channel_id=1, source_target_pairs={{0,8},{4,12},{8,16},{12,20},{16,24},{20,28},{24,0},{28,4},{1,9},{5... | collective-permute-start | bytes 393224 | tf_op jit(solution)/shard_map/ppermute | solution.py:197
  67.7 7.7 %collective-permute-start.35 = (f32[64,256]{1,0:T(8,128)S(1)}, f32[64,256]{1,0:T(8,128)S(1)}, u32[]{:S(2)}, u32[]{:S(2)}) collective-permute-start(f32[64,256]{1,0:T(8,128)S(1)} %add.118), channel_id=1, source_target_pairs={{0,64},{32,96},{64,0},{96,32},{128,192},{160,224},{192,128},{224,1... | collective-permute-start | bytes 196616 | tf_op jit(solution)/shard_map/ppermute | solution.py:202
  69.0 8.5 %collective-permute-start.23 = (f32[64,512]{1,0:T(8,128)S(1)}, f32[64,512]{1,0:T(8,128)S(1)}, u32[]{:S(2)}, u32[]{:S(2)}) collective-permute-start(f32[64,512]{1,0:T(8,128)S(1)} %get-tuple-element.39.refs_0_), channel_id=1, source_target_pairs={{0,16},{4,20},{8,24},{12,28},{16,0},{20,4},{24,8},{28,12},{1,17},{... | collective-permute-start | bytes 393224 | tf_op jit(solution)/shard_map/ppermute | solution.py:197
  70.1 14.0 %collective-permute-start.21 = (f32[64,512]{1,0:T(8,128)S(1)}, f32[64,512]{1,0:T(8,128)S(1)}, u32[]{:S(2)}, u32[]{:S(2)}) collective-permute-start(f32[64,512]{1,0:T(8,128)S(1)} %get-tuple-element.39.refs_0_), channel_id=1, source_target_pairs={{0,24},{4,28},{8,0},{12,4},{16,8},{20,12},{24,16},{28,20},{1,25},{... | collective-permute-start | bytes 393224 | tf_op jit(solution)/shard_map/ppermute | solution.py:197
  72.8 11.4 %collective-permute-start.26 = (f32[64,512]{1,0:T(8,128)S(1)}, f32[64,512]{1,0:T(8,128)S(1)}, u32[]{:S(2)}, u32[]{:S(2)}) collective-permute-start(f32[64,512]{1,0:T(8,128)S(1)} %collective-permute-done.20.refs_1_), channel_id=1, source_target_pairs={{0,8},{4,12},{8,16},{12,20},{16,24},{20,28},{24,0},{28,4},{1,9},{5... | collective-permute-start | bytes 393224 | tf_op jit(solution)/shard_map/ppermute | solution.py:197
  75.5 8.7 %collective-permute-start.24 = (f32[64,512]{1,0:T(8,128)S(1)}, f32[64,512]{1,0:T(8,128)S(1)}, u32[]{:S(2)}, u32[]{:S(2)}) collective-permute-start(f32[64,512]{1,0:T(8,128)S(1)} %collective-permute-done.20.refs_1_), channel_id=1, source_target_pairs={{0,16},{4,20},{8,24},{12,28},{16,0},{20,4},{24,8},{28,12},{1,17},{... | collective-permute-start | bytes 393224 | tf_op jit(solution)/shard_map/ppermute | solution.py:197
  77.4 7.0 %collective-permute-start.22 = (f32[64,512]{1,0:T(8,128)S(1)}, f32[64,512]{1,0:T(8,128)S(1)}, u32[]{:S(2)}, u32[]{:S(2)}) collective-permute-start(f32[64,512]{1,0:T(8,128)S(1)} %collective-permute-done.20.refs_1_), channel_id=1, source_target_pairs={{0,24},{4,28},{8,0},{12,4},{16,8},{20,12},{24,16},{28,20},{1,25},{... | collective-permute-start | bytes 393224 | tf_op jit(solution)/shard_map/ppermute | solution.py:197
  77.6 13.3 %collective-permute-start.36 = (f32[64,256]{1,0:T(8,128)S(1)}, f32[64,256]{1,0:T(8,128)S(1)}, u32[]{:S(2)}, u32[]{:S(2)}) collective-permute-start(f32[64,256]{1,0:T(8,128)S(1)} %add.119), channel_id=1, source_target_pairs={{0,128},{32,160},{64,192},{96,224},{128,0},{160,32},{192,64},{224,... | collective-permute-start | bytes 196616 | tf_op jit(solution)/shard_map/ppermute | solution.py:202
  90.2 12.3 %collective-permute-start.28 = (f32[64,512]{1,0:T(8,128)S(1)}, f32[64,512]{1,0:T(8,128)S(1)}, u32[]{:S(2)}, u32[]{:S(2)}) collective-permute-start(f32[64,512]{1,0:T(8,128)S(1)} %get-tuple-element.43), channel_id=1, source_target_pairs={{0,32},{32,0},{64,96},{96,64},{128,160},{160,128},{192,224},{224,1... | collective-permute-start | bytes 393224 | tf_op jit(solution)/shard_map/ppermute | solution.py:202
  90.3 15.8 %collective-permute-start.30 = (f32[64,512]{1,0:T(8,128)S(1)}, f32[64,512]{1,0:T(8,128)S(1)}, u32[]{:S(2)}, u32[]{:S(2)}) collective-permute-start(f32[64,512]{1,0:T(8,128)S(1)} %get-tuple-element.45), channel_id=1, source_target_pairs={{0,32},{32,0},{64,96},{96,64},{128,160},{160,128},{192,224},{224,1... | collective-permute-start | bytes 393224 | tf_op jit(solution)/shard_map/ppermute | solution.py:202
  90.8 17.2 %collective-permute-start.32 = (f32[64,512]{1,0:T(8,128)S(1)}, f32[64,512]{1,0:T(8,128)S(1)}, u32[]{:S(2)}, u32[]{:S(2)}) collective-permute-start(f32[64,512]{1,0:T(8,128)S(1)} %get-tuple-element.47), channel_id=1, source_target_pairs={{0,32},{32,0},{64,96},{96,64},{128,160},{160,128},{192,224},{224,1... | collective-permute-start | bytes 393224 | tf_op jit(solution)/shard_map/ppermute | solution.py:202
  90.9 8.5 %collective-permute-start.37 = (f32[64,256]{1,0:T(8,128)S(1)}, f32[64,256]{1,0:T(8,128)S(1)}, u32[]{:S(2)}, u32[]{:S(2)}) collective-permute-start(f32[64,256]{1,0:T(8,128)S(1)} %add.120), channel_id=1, source_target_pairs={{0,4},{4,0},{8,12},{12,8},{16,20},{20,16},{24,28},{28,24},{1,5},{5... | collective-permute-start | bytes 196616 | tf_op jit(solution)/shard_map/ppermute | solution.py:202
  99.4 10.1 %collective-permute-start.38 = (f32[64,256]{1,0:T(8,128)S(1)}, f32[64,256]{1,0:T(8,128)S(1)}, u32[]{:S(2)}, u32[]{:S(2)}) collective-permute-start(f32[64,256]{1,0:T(8,128)S(1)} %add.121), channel_id=1, source_target_pairs={{0,8},{4,12},{8,0},{12,4},{16,24},{20,28},{24,16},{28,20},{1,9},{5... | collective-permute-start | bytes 196616 | tf_op jit(solution)/shard_map/ppermute | solution.py:202
  102.4 13.6 %collective-permute-start.27 = (f32[64,512]{1,0:T(8,128)S(1)}, f32[64,512]{1,0:T(8,128)S(1)}, u32[]{:S(2)}, u32[]{:S(2)}) collective-permute-start(f32[64,512]{1,0:T(8,128)S(1)} %get-tuple-element.41), channel_id=1, source_target_pairs={{0,32},{32,0},{64,96},{96,64},{128,160},{160,128},{192,224},{224,1... | collective-permute-start | bytes 393224 | tf_op jit(solution)/shard_map/ppermute | solution.py:202
  102.4 13.6 %collective-permute-start.29 = (f32[64,512]{1,0:T(8,128)S(1)}, f32[64,512]{1,0:T(8,128)S(1)}, u32[]{:S(2)}, u32[]{:S(2)}) collective-permute-start(f32[64,512]{1,0:T(8,128)S(1)} %add.112), channel_id=1, source_target_pairs={{0,128},{32,160},{64,192},{96,224},{128,0},{160,32},{192,64},{224,... | collective-permute-start | bytes 393224 | tf_op jit(solution)/shard_map/ppermute | solution.py:197
  106.1 9.9 %collective-permute-start.31 = (f32[64,512]{1,0:T(8,128)S(1)}, f32[64,512]{1,0:T(8,128)S(1)}, u32[]{:S(2)}, u32[]{:S(2)}) collective-permute-start(f32[64,512]{1,0:T(8,128)S(1)} %add.114), channel_id=1, source_target_pairs={{0,64},{32,96},{64,128},{96,160},{128,192},{160,224},{192,0},{224,... | collective-permute-start | bytes 393224 | tf_op jit(solution)/shard_map/ppermute | solution.py:197
  108.0 8.1 %collective-permute-start.33 = (f32[64,512]{1,0:T(8,128)S(1)}, f32[64,512]{1,0:T(8,128)S(1)}, u32[]{:S(2)}, u32[]{:S(2)}) collective-permute-start(f32[64,512]{1,0:T(8,128)S(1)} %add.116), channel_id=1, source_target_pairs={{0,192},{32,224},{64,0},{96,32},{128,64},{160,96},{192,128},{224,1... | collective-permute-start | bytes 393224 | tf_op jit(solution)/shard_map/ppermute | solution.py:197
  (11 other events, 135.2 us)
where the time goes:
time: 119 us; the launch traced here: 117 us
  starting transfers between devices  75.1 us (63%)
  waiting for transfers between devices  23 us (19%)
  Pallas kernels  13.2 us (11%)
  other arithmetic  2.26 us (2%)
  local copies, waits for them, and re-layouts  1.74 us (1%)
  between operations  1.48 us (1%)
    ppermute x22, starting transfers between devices, swap(): return lax.ppermute(x, axis, [(i, i ^ bit) for i in range(n)])  41.1 us
    ppermute x18, starting transfers between devices, shift(): return lax.ppermute(x, axis, [(i, (i + by) % n) for i in range(n)])  34 us
    ppermute x22, waiting for transfers between devices, swap(): return lax.ppermute(x, axis, [(i, i ^ bit) for i in range(n)])  18.9 us
    pallas_call x2, Pallas kernels, spmm(): pl.pallas_call(functools.partial(spmm_kernel, transposed, n_in, n_out), i...  11.4 us
    ppermute x18, waiting for transfers between devices, shift(): return lax.ppermute(x, axis, [(i, (i + by) % n) for i in range(n)])  4.12 us
  transfers between devices with their start and end apart: 40, of which 10 were waited for; matrix products, arithmetic and copies ran while one was open for 2% of the time, Pallas kernels for 5%

commit v1 on v0

--- a/solution.py
+++ b/solution.py
@@ -13,7 +13,6 @@
 NT = (((1,), (1,)), ((), ()))
 NN = (((1,), (0,)), ((), ()))
 GROUP = 16
-RING = 4
 ROOT_2_PI = 0.7978845608028654
 CUBIC = 0.044715
 
@@ -35,31 +34,12 @@
     sources = refs[:n_in]
     values = refs[n_in]
     outs = refs[n_in + 1 : n_in + 1 + n_out]
-    buf, sem, held, acc = refs[n_in + 1 + n_out :]
+    held, acc = refs[n_in + 1 + n_out :]
     width, length = sources[0].shape
     edge = values.shape[-1]
     per = length // edge
     to_row, from_row = (2, 3) if transposed else (0, 1)
     groups = (table[5, 0] + GROUP - 1) // GROUP
-
-    def copy(group, u):
-        slot = lax.rem(group, RING)
-        return pltpu.make_async_copy(
-            values.at[table[4, group * GROUP + u]], buf.at[slot, u], sem.at[slot, u]
-        )
-
-    def start(group):
-        def one(u, carry):
-            copy(group, u).start()
-            return carry
-
-        lax.fori_loop(0, GROUP, one, 0, unroll=4)
-
-    for g in range(RING - 1):
-
-        @pl.when(g < groups)
-        def _():
-            start(g)
 
     for b in range(n_in):
         for j in range(per):
@@ -69,17 +49,10 @@
     acc[...] = jnp.zeros_like(acc)
 
     def step(group, carry):
-        @pl.when(group + RING - 1 < groups)
-        def _():
-            start(group + RING - 1)
-
-        for u in range(GROUP):
-            copy(group, u).wait()
-        slot = lax.rem(group, RING)
         products = []
         for u in range(GROUP):
             both = held[table[from_row, group * GROUP + u]]
-            high, low = split(buf[slot, u])
+            high, low = split(values[table[4, group * GROUP + u]])
             if transposed:
                 p = dot(both, high, NN)
                 products.append(p[:width] + p[width:] + dot(both[:width], low, NN))
@@ -107,16 +80,14 @@
         functools.partial(spmm_kernel, transposed, n_in, n_out),
         in_specs=[pl.BlockSpec(memory_space=pltpu.SMEM)]
         + [vmem] * n_in
-        + [pl.BlockSpec(memory_space=pl.ANY)],
+        + [vmem],
         out_specs=[vmem] * n_out,
         out_shape=[jax.ShapeDtypeStruct((width, length), F32)] * n_out,
         scratch_shapes=[
-            pltpu.VMEM((RING, GROUP, edge, edge), F32),
-            pltpu.SemaphoreType.DMA((RING, GROUP)),
             pltpu.VMEM((n_in * per, 2 * width, edge), BF16),
             pltpu.VMEM((n_out * per + 1, width, edge), F32),
         ],
-        compiler_params=pltpu.CompilerParams(vmem_limit_bytes=51 << 20),
+        compiler_params=pltpu.CompilerParams(vmem_limit_bytes=24 << 20),
         cost_estimate=pl.CostEstimate(
             flops=6 * slots * width * edge * edge, bytes_accessed=14 << 20, transcendentals=0
         ),
@@ -231,23 +202,27 @@
     for k in range(n_row // 2):
         mine = features if k == 0 else shift(features, "row", -2 * k)
         blocks += [mine, swap(mine, "row", 1)]
-    cots = [cotangent] + [swap(cotangent, "rep", k) for k in range(1, n_rep)]
-    table, *cots[1:] = lax.optimization_barrier((table, *cots[1:]))
+    cots = [cotangent]
+    for k in range(1, n_rep):
+        cots.append(swap(cotangent, "rep", k))
     parts = spmm(table, blocks, tile_values, n_col, False)
     sums = [None, None]
     for z in (1, 0):
         total = parts[z]
         for k in range(1, n_col // 2):
-            total = total + shift(parts[2 * k + z], "col", 2 * k)
+            got = shift(parts[2 * k + z], "col", 2 * k)
+            total = total + got
         sums[z] = total
-    agg = sums[0] + swap(sums[1], "col", 1)
+    far = swap(sums[1], "col", 1)
+    agg = sums[0] + far
     aggs = [agg] + [swap(agg, "rep", k) for k in range(1, n_rep)]
     place = rep.astype(jnp.int32)[None]
     output, mixed_grad, grad_pre = mid(place, aggs, cots, weight, weight.T)
     far = swap(mixed_grad, "col", 1)
     blocks = [mixed_grad, far]
     for k in range(1, n_col // 2):
-        blocks += [shift(mixed_grad, "col", -2 * k), shift(far, "col", -2 * k)]
+        blocks.append(shift(mixed_grad, "col", -2 * k))
+        blocks.append(shift(far, "col", -2 * k))
     node_total = stretch * n_row * n_col
     weight_grad = weight_part(agg, grad_pre, float(node_total) ** (-0.5))
 

time: 119 us -> 127 us (1.067)
  the two profiles are of different devices: /device:TPU:2 before, /device:TPU:35 now
where the time goes in v1:
time: 127 us
  starting transfers between devices  62.9 us (50%)
  waiting for transfers between devices  43.5 us (34%)
  local copies, waits for them, and re-layouts  9.7 us (8%)
  Pallas kernels  7.31 us (6%)
  other arithmetic  2.27 us (2%)
  between operations  1.5 us (1%)
    ppermute x22, waiting for transfers between devices, swap(): return lax.ppermute(x, axis, [(i, i ^ bit) for i in range(n)])  35.6 us
    ppermute x22, starting transfers between devices, swap(): return lax.ppermute(x, axis, [(i, i ^ bit) for i in range(n)])  35.5 us
    ppermute x18, starting transfers between devices, shift(): return lax.ppermute(x, axis, [(i, (i + by) % n) for i in range(n)])  27.3 us
    unnamed x11, local copies, waits for them, and re-layouts  8.99 us
    ppermute x18, waiting for transfers between devices, shift(): return lax.ppermute(x, axis, [(i, (i + by) % n) for i in range(n)])  7.9 us
    pallas_call x2, Pallas kernels, spmm(): pl.pallas_call(functools.partial(spmm_kernel, transposed, n_in, n_out), i...  5.54 us
  transfers between devices with their start and end apart: 40, of which 14 were waited for; matrix products, arithmetic and copies ran while one was open for 2% of the time, Pallas kernels for 2%

profile of v1, /device:TPU:35, one launch (start us, length us, event | category | flops | bytes accessed | tf_op | source)
XLA Modules:
  0.0 127.2 jit_solution(12228026460254133763)
XLA Ops:
  0.6 2.8 %collective-permute-start.1 = (f32[64,512]{1,0:T(8,128)}, f32[64,512]{1,0:T(8,128)S(1)}, u32[]{:S(2)}, u32[]{:S(2)}) collective-permute-start(f32[64,512]{1,0:T(8,128)} %refs_0_.1), channel_id=1, source_target_pairs={{0,192},{32,224},{64,0},{96,32},{128,64},{160,96},{192,128},{224,1... | collective-permute-start | bytes 393224 | tf_op jit(solution)/shard_map/ppermute | solution.py:168
  4.5 1.5 %collective-permute-start = (f32[64,512]{1,0:T(8,128)}, f32[64,512]{1,0:T(8,128)S(1)}, u32[]{:S(2)}, u32[]{:S(2)}) collective-permute-start(f32[64,512]{1,0:T(8,128)} %refs_0_.1), channel_id=1, source_target_pairs={{0,32},{32,0},{64,96},{96,64},{128,160},{160,128},{192,224},{224,1... | collective-permute-start | bytes 393224 | tf_op jit(solution)/shard_map/ppermute | solution.py:173
  6.7 2.1 %collective-permute-done.1.refs_2_ = f32[64,512]{1,0:T(8,128)S(1)} collective-permute-done((f32[64,512]{1,0:T(8,128)}, f32[64,512]{1,0:T(8,128)S(1)}, u32[]{:S(2)}, u32[]{:S(2)}) %collective-permute-start.1) | collective-permute-done | bytes 131104 | tf_op jit(solution)/shard_map/ppermute | solution.py:168
  8.8 1.5 %collective-permute-start.2 = (f32[64,512]{1,0:T(8,128)S(1)}, f32[64,512]{1,0:T(8,128)S(1)}, u32[]{:S(2)}, u32[]{:S(2)}) collective-permute-start(f32[64,512]{1,0:T(8,128)S(1)} %collective-permute-done.1.refs_2_), channel_id=1, source_target_pairs={{0,32},{32,0},{64,96},{96,64},{128,160},{160,128},{192,224},{224,1... | collective-permute-start | bytes 393224 | tf_op jit(solution)/shard_map/ppermute | solution.py:173
  10.3 2.2 %collective-permute-start.4 = (f32[64,512]{1,0:T(8,128)S(1)}, f32[64,512]{1,0:T(8,128)S(1)}, u32[]{:S(2)}, u32[]{:S(2)}) collective-permute-start(f32[64,512]{1,0:T(8,128)S(1)} %collective-permute-done.3.refs_4_), channel_id=1, source_target_pairs={{0,32},{32,0},{64,96},{96,64},{128,160},{160,128},{192,224},{224,1... | collective-permute-start | bytes 393224 | tf_op jit(solution)/shard_map/ppermute | solution.py:173
  15.4 4.0 %copy-done = f32[160,128,128]{2,1,0:T(8,128)S(1)} copy-done((f32[160,128,128]{2,1,0:T(8,128)S(1)}, f32[160,128,128]{2,1,0:T(8,128)}, u32[]{:S(2)}) %copy-start) | copy-done | bytes 10485784
  20.2 2.8 %spmm.1 = (f32[64,512]{1,0:T(8,128)S(1)}, f32[64,512]{1,0:T(8,128)S(1)}, f32[64,512]{1,0:T(8,128)S(1)}, f32[64,512]{1,0:T(8,128)S(1)}, f32[64,512]{1,0:T(8,128)S...) custom-call(s32[6,160]{1,0:T(8,128)S(1)} %stack.23.table, f32[64,512]{1,0:T(8,128)S(1)} %copy-done.3, ...), custom_call_target="tpu_custom_call" | custom-call | flops 1006632960 | bytes 14680064 | tf_op jit(solution)/shard_map/spmm/pallas_call | solution.py:79
  23.0 1.8 %collective-permute-start.10 = (f32[64,512]{1,0:T(8,128)S(1)}, f32[64,512]{1,0:T(8,128)S(1)}, u32[]{:S(2)}, u32[]{:S(2)}) collective-permute-start(f32[64,512]{1,0:T(8,128)S(1)} %get-tuple-element.27), channel_id=1, source_target_pairs={{0,8},{4,12},{8,16},{12,20},{16,24},{20,28},{24,0},{28,4},{1,9},{5... | collective-permute-start | bytes 393224 | tf_op jit(solution)/shard_map/ppermute | solution.py:168
  24.8 3.1 %collective-permute-start.11 = (f32[64,512]{1,0:T(8,128)S(1)}, f32[64,512]{1,0:T(8,128)S(1)}, u32[]{:S(2)}, u32[]{:S(2)}) collective-permute-start(f32[64,512]{1,0:T(8,128)S(1)} %get-tuple-element.28), channel_id=1, source_target_pairs={{0,16},{4,20},{8,24},{12,28},{16,0},{20,4},{24,8},{28,12},{1,17},{... | collective-permute-start | bytes 393224 | tf_op jit(solution)/shard_map/ppermute | solution.py:168
  27.9 1.5 %collective-permute-start.7 = (f32[64,512]{1,0:T(8,128)S(1)}, f32[64,512]{1,0:T(8,128)S(1)}, u32[]{:S(2)}, u32[]{:S(2)}) collective-permute-start(f32[64,512]{1,0:T(8,128)S(1)} %get-tuple-element.23), channel_id=1, source_target_pairs={{0,8},{4,12},{8,16},{12,20},{16,24},{20,28},{24,0},{28,4},{1,9},{5... | collective-permute-start | bytes 393224 | tf_op jit(solution)/shard_map/ppermute | solution.py:168
  30.6 4.6 %collective-permute-start.9 = (f32[64,512]{1,0:T(8,128)S(1)}, f32[64,512]{1,0:T(8,128)S(1)}, u32[]{:S(2)}, u32[]{:S(2)}) collective-permute-start(f32[64,512]{1,0:T(8,128)S(1)} %get-tuple-element.25), channel_id=1, source_target_pairs={{0,24},{4,28},{8,0},{12,4},{16,8},{20,12},{24,16},{28,20},{1,25},{... | collective-permute-start | bytes 393224 | tf_op jit(solution)/shard_map/ppermute | solution.py:168
  35.3 6.6 %collective-permute-start.13 = (f32[64,512]{1,0:T(8,128)S(1)}, f32[64,512]{1,0:T(8,128)S(1)}, u32[]{:S(2)}, u32[]{:S(2)}) collective-permute-start(f32[64,512]{1,0:T(8,128)S(1)} %add_add_fusion.1), channel_id=1, source_target_pairs={{0,4},{4,0},{8,12},{12,8},{16,20},{20,16},{24,28},{28,24},{1,5},{5... | collective-permute-start | bytes 393224 | tf_op jit(solution)/shard_map/ppermute | solution.py:173
  44.6 3.0 %collective-permute-done.13 = f32[64,512]{1,0:T(8,128)S(1)} collective-permute-done((f32[64,512]{1,0:T(8,128)S(1)}, f32[64,512]{1,0:T(8,128)S(1)}, u32[]{:S(2)}, u32[]{:S(2)}) %collective-permute-start.13) | collective-permute-done | bytes 131104 | tf_op jit(solution)/shard_map/ppermute | solution.py:173
  47.7 3.4 %collective-permute-start.15 = (f32[64,512]{1,0:T(8,128)S(1)}, f32[64,512]{1,0:T(8,128)S(1)}, u32[]{:S(2)}, u32[]{:S(2)}) collective-permute-start(f32[64,512]{1,0:T(8,128)S(1)} %add_add_fusion.2.refs_0_.agg), channel_id=1, source_target_pairs={{0,2},{1,3},{2,0},{3,1},{4,6},{5,7},{6,4},{7,5},{8,10},{9,11},{10,... | collective-permute-start | bytes 393224 | tf_op jit(solution)/shard_map/ppermute | solution.py:173
  51.1 1.5 %collective-permute-done.17.refs_5_ = f32[64,512]{1,0:T(8,128)S(1)} collective-permute-done((f32[64,512]{1,0:T(8,128)S(1)}, f32[64,512]{1,0:T(8,128)S(1)}, u32[]{:S(2)}, u32[]{:S(2)}) %collective-permute-start.17) | collective-permute-done | bytes 131104 | tf_op jit(solution)/shard_map/ppermute | solution.py:173
  53.7 6.7 %collective-permute-done.19.refs_7_ = f32[64,512]{1,0:T(8,128)S(1)} collective-permute-done((f32[64,512]{1,0:T(8,128)S(1)}, f32[64,512]{1,0:T(8,128)S(1)}, u32[]{:S(2)}, u32[]{:S(2)}) %collective-permute-start.19) | collective-permute-done | bytes 131104 | tf_op jit(solution)/shard_map/ppermute | solution.py:173
  60.4 6.4 %collective-permute-done.15.refs_2_ = f32[64,512]{1,0:T(8,128)S(1)} collective-permute-done((f32[64,512]{1,0:T(8,128)S(1)}, f32[64,512]{1,0:T(8,128)S(1)}, u32[]{:S(2)}, u32[]{:S(2)}) %collective-permute-start.15) | collective-permute-done | bytes 131104 | tf_op jit(solution)/shard_map/ppermute | solution.py:173
  66.8 4.3 %collective-permute-done.16.refs_3_ = f32[64,512]{1,0:T(8,128)S(1)} collective-permute-done((f32[64,512]{1,0:T(8,128)S(1)}, f32[64,512]{1,0:T(8,128)S(1)}, u32[]{:S(2)}, u32[]{:S(2)}) %collective-permute-start.16) | collective-permute-done | bytes 131104 | tf_op jit(solution)/shard_map/ppermute | solution.py:173
  71.1 1.4 %mid.1 = (f32[64,512]{1,0:T(8,128)}, f32[64,512]{1,0:T(8,128)S(1)}, f32[256,512]{1,0:T(8,128)S(1)}) custom-call(s32[1]{0:T(128)} %bitcast.place, f32[64,512]{1,0:T(8,128)S(1)} %add_add_fusion.2.refs_0_.agg, f32[64,512]{1,0:T(8,128)S(1)} %collective-permute-done.14.refs_1_, f32[64,512]{1,0:T(8,128)S(1)} %collective-permute-done.15.refs_2_, ...), custom_call_target="tpu_custom_call" | custom-call | flops 268435456 | bytes 4194304 | tf_op jit(solution)/shard_map/mid/pallas_call | solution.py:129
  73.6 1.8 %collective-permute-start.20 = (f32[64,512]{1,0:T(8,128)S(1)}, f32[64,512]{1,0:T(8,128)S(1)}, u32[]{:S(2)}, u32[]{:S(2)}) collective-permute-start(f32[64,512]{1,0:T(8,128)S(1)} %get-tuple-element.31.refs_0_), channel_id=1, source_target_pairs={{0,4},{4,0},{8,12},{12,8},{16,20},{20,16},{24,28},{28,24},{1,5},{5... | collective-permute-start | bytes 393224 | tf_op jit(solution)/shard_map/ppermute | solution.py:173
  77.9 2.1 %collective-permute-start.25 = (f32[64,512]{1,0:T(8,128)S(1)}, f32[64,512]{1,0:T(8,128)S(1)}, u32[]{:S(2)}, u32[]{:S(2)}) collective-permute-start(f32[64,512]{1,0:T(8,128)S(1)} %get-tuple-element.31.refs_0_), channel_id=1, source_target_pairs={{0,8},{4,12},{8,16},{12,20},{16,24},{20,28},{24,0},{28,4},{1,9},{5... | collective-permute-start | bytes 393224 | tf_op jit(solution)/shard_map/ppermute | solution.py:168
  80.0 5.0 %collective-permute-done.20.refs_1_ = f32[64,512]{1,0:T(8,128)S(1)} collective-permute-done((f32[64,512]{1,0:T(8,128)S(1)}, f32[64,512]{1,0:T(8,128)S(1)}, u32[]{:S(2)}, u32[]{:S(2)}) %collective-permute-start.20) | collective-permute-done | bytes 131104 | tf_op jit(solution)/shard_map/ppermute | solution.py:173
  86.7 2.1 %collective-permute-start.26 = (f32[64,512]{1,0:T(8,128)S(1)}, f32[64,512]{1,0:T(8,128)S(1)}, u32[]{:S(2)}, u32[]{:S(2)}) collective-permute-start(f32[64,512]{1,0:T(8,128)S(1)} %collective-permute-done.20.refs_1_), channel_id=1, source_target_pairs={{0,8},{4,12},{8,16},{12,20},{16,24},{20,28},{24,0},{28,4},{1,9},{5... | collective-permute-start | bytes 393224 | tf_op jit(solution)/shard_map/ppermute | solution.py:168
  89.8 3.1 %collective-permute-done.24.refs_5_ = f32[64,512]{1,0:T(8,128)S(1)} collective-permute-done((f32[64,512]{1,0:T(8,128)S(1)}, f32[64,512]{1,0:T(8,128)S(1)}, u32[]{:S(2)}, u32[]{:S(2)}) %collective-permute-start.24) | collective-permute-done | bytes 131104 | tf_op jit(solution)/shard_map/ppermute | solution.py:168
  93.9 4.0 %copy-done.1 = f32[160,128,128]{2,1,0:T(8,128)S(1)} copy-done((f32[160,128,128]{2,1,0:T(8,128)S(1)}, f32[160,128,128]{2,1,0:T(8,128)}, u32[]{:S(2)}) %copy-start.1) | copy-done | bytes 10485784
  97.9 2.8 %spmm_back.1 = (f32[64,512]{1,0:T(8,128)S(1)}, f32[64,512]{1,0:T(8,128)S(1)}, f32[64,512]{1,0:T(8,128)S(1)}, f32[64,512]{1,0:T(8,128)S(1)}, f32[64,512]{1,0:T(8,...) custom-call(s32[6,160]{1,0:T(8,128)S(1)} %stack.23.table, ...), custom_call_target="tpu_custom_call" | custom-call | flops 1006632960 | bytes 14680064 | tf_op jit(solution)/shard_map/spmm_back/pallas_call | solution.py:79
  100.6 2.6 %collective-permute-start.28 = (f32[64,512]{1,0:T(8,128)S(1)}, f32[64,512]{1,0:T(8,128)S(1)}, u32[]{:S(2)}, u32[]{:S(2)}) collective-permute-start(f32[64,512]{1,0:T(8,128)S(1)} %get-tuple-element.35), channel_id=1, source_target_pairs={{0,32},{32,0},{64,96},{96,64},{128,160},{160,128},{192,224},{224,1... | collective-permute-start | bytes 393224 | tf_op jit(solution)/shard_map/ppermute | solution.py:173
  103.7 3.4 %collective-permute-start.37 = (f32[64,256]{1,0:T(8,128)S(1)}, f32[64,256]{1,0:T(8,128)S(1)}, u32[]{:S(2)}, u32[]{:S(2)}) collective-permute-start(f32[64,256]{1,0:T(8,128)S(1)} %add.120), channel_id=1, source_target_pairs={{0,4},{4,0},{8,12},{12,8},{16,20},{20,16},{24,28},{28,24},{1,5},{5... | collective-permute-start | bytes 196616 | tf_op jit(solution)/shard_map/ppermute | solution.py:173
  107.2 4.1 %collective-permute-done.37 = f32[64,256]{1,0:T(8,128)S(1)} collective-permute-done((f32[64,256]{1,0:T(8,128)S(1)}, f32[64,256]{1,0:T(8,128)S(1)}, u32[]{:S(2)}, u32[]{:S(2)}) %collective-permute-start.37) | collective-permute-done | bytes 65568 | tf_op jit(solution)/shard_map/ppermute | solution.py:173
  111.3 4.2 %collective-permute-start.38 = (f32[64,256]{1,0:T(8,128)S(1)}, f32[64,256]{1,0:T(8,128)S(1)}, u32[]{:S(2)}, u32[]{:S(2)}) collective-permute-start(f32[64,256]{1,0:T(8,128)S(1)} %add.121), channel_id=1, source_target_pairs={{0,8},{4,12},{8,0},{12,4},{16,24},{20,28},{24,16},{28,20},{1,9},{5... | collective-permute-start | bytes 196616 | tf_op jit(solution)/shard_map/ppermute | solution.py:173
  117.3 2.7 %collective-permute-start.33 = (f32[64,512]{1,0:T(8,128)S(1)}, f32[64,512]{1,0:T(8,128)S(1)}, u32[]{:S(2)}, u32[]{:S(2)}) collective-permute-start(f32[64,512]{1,0:T(8,128)S(1)} %add.116), channel_id=1, source_target_pairs={{0,192},{32,224},{64,0},{96,32},{128,64},{160,96},{192,128},{224,1... | collective-permute-start | bytes 393224 | tf_op jit(solution)/shard_map/ppermute | solution.py:168
  120.7 4.3 %collective-permute-done.39 = f32[64,256]{1,0:T(8,128)S(1)} collective-permute-done((f32[64,256]{1,0:T(8,128)S(1)}, f32[64,256]{1,0:T(8,128)S(1)}, u32[]{:S(2)}, u32[]{:S(2)}) %collective-permute-start.39) | collective-permute-done | bytes 65568 | tf_op jit(solution)/shard_map/ppermute | solution.py:173
  (78 shorter events, 22.4 us)
Async XLA Ops:
  0.6 8.2 %collective-permute-start.1 = (f32[64,512]{1,0:T(8,128)}, f32[64,512]{1,0:T(8,128)S(1)}, u32[]{:S(2)}, u32[]{:S(2)}) collective-permute-start(f32[64,512]{1,0:T(8,128)} %refs_0_.1), channel_id=1, source_target_pairs={{0,192},{32,224},{64,0},{96,32},{128,64},{160,96},{192,128},{224,1... | collective-permute-start | bytes 393224 | tf_op jit(solution)/shard_map/ppermute | solution.py:168
  3.8 9.5 %collective-permute-start.5 = (f32[64,512]{1,0:T(8,128)}, f32[64,512]{1,0:T(8,128)S(1)}, u32[]{:S(2)}, u32[]{:S(2)}) collective-permute-start(f32[64,512]{1,0:T(8,128)} %refs_0_.1), channel_id=1, source_target_pairs={{0,64},{32,96},{64,128},{96,160},{128,192},{160,224},{192,0},{224,... | collective-permute-start | bytes 393224 | tf_op jit(solution)/shard_map/ppermute | solution.py:168
  4.5 10.8 %collective-permute-start = (f32[64,512]{1,0:T(8,128)}, f32[64,512]{1,0:T(8,128)S(1)}, u32[]{:S(2)}, u32[]{:S(2)}) collective-permute-start(f32[64,512]{1,0:T(8,128)} %refs_0_.1), channel_id=1, source_target_pairs={{0,32},{32,0},{64,96},{96,64},{128,160},{160,128},{192,224},{224,1... | collective-permute-start | bytes 393224 | tf_op jit(solution)/shard_map/ppermute | solution.py:173
  23.0 7.6 %collective-permute-start.10 = (f32[64,512]{1,0:T(8,128)S(1)}, f32[64,512]{1,0:T(8,128)S(1)}, u32[]{:S(2)}, u32[]{:S(2)}) collective-permute-start(f32[64,512]{1,0:T(8,128)S(1)} %get-tuple-element.27), channel_id=1, source_target_pairs={{0,8},{4,12},{8,16},{12,20},{16,24},{20,28},{24,0},{28,4},{1,9},{5... | collective-permute-start | bytes 393224 | tf_op jit(solution)/shard_map/ppermute | solution.py:168
  24.8 10.5 %collective-permute-start.11 = (f32[64,512]{1,0:T(8,128)S(1)}, f32[64,512]{1,0:T(8,128)S(1)}, u32[]{:S(2)}, u32[]{:S(2)}) collective-permute-start(f32[64,512]{1,0:T(8,128)S(1)} %get-tuple-element.28), channel_id=1, source_target_pairs={{0,16},{4,20},{8,24},{12,28},{16,0},{20,4},{24,8},{28,12},{1,17},{... | collective-permute-start | bytes 393224 | tf_op jit(solution)/shard_map/ppermute | solution.py:168
  27.9 7.3 %collective-permute-start.12 = (f32[64,512]{1,0:T(8,128)S(1)}, f32[64,512]{1,0:T(8,128)S(1)}, u32[]{:S(2)}, u32[]{:S(2)}) collective-permute-start(f32[64,512]{1,0:T(8,128)S(1)} %get-tuple-element.29), channel_id=1, source_target_pairs={{0,24},{4,28},{8,0},{12,4},{16,8},{20,12},{24,16},{28,20},{1,25},{... | collective-permute-start | bytes 393224 | tf_op jit(solution)/shard_map/ppermute | solution.py:168
  27.9 14.7 %collective-permute-start.7 = (f32[64,512]{1,0:T(8,128)S(1)}, f32[64,512]{1,0:T(8,128)S(1)}, u32[]{:S(2)}, u32[]{:S(2)}) collective-permute-start(f32[64,512]{1,0:T(8,128)S(1)} %get-tuple-element.23), channel_id=1, source_target_pairs={{0,8},{4,12},{8,16},{12,20},{16,24},{20,28},{24,0},{28,4},{1,9},{5... | collective-permute-start | bytes 393224 | tf_op jit(solution)/shard_map/ppermute | solution.py:168
  29.4 14.4 %collective-permute-start.8 = (f32[64,512]{1,0:T(8,128)S(1)}, f32[64,512]{1,0:T(8,128)S(1)}, u32[]{:S(2)}, u32[]{:S(2)}) collective-permute-start(f32[64,512]{1,0:T(8,128)S(1)} %get-tuple-element.24), channel_id=1, source_target_pairs={{0,16},{4,20},{8,24},{12,28},{16,0},{20,4},{24,8},{28,12},{1,17},{... | collective-permute-start | bytes 393224 | tf_op jit(solution)/shard_map/ppermute | solution.py:168
  30.6 14.0 %collective-permute-start.9 = (f32[64,512]{1,0:T(8,128)S(1)}, f32[64,512]{1,0:T(8,128)S(1)}, u32[]{:S(2)}, u32[]{:S(2)}) collective-permute-start(f32[64,512]{1,0:T(8,128)S(1)} %get-tuple-element.25), channel_id=1, source_target_pairs={{0,24},{4,28},{8,0},{12,4},{16,8},{20,12},{24,16},{28,20},{1,25},{... | collective-permute-start | bytes 393224 | tf_op jit(solution)/shard_map/ppermute | solution.py:168
  35.3 12.2 %collective-permute-start.13 = (f32[64,512]{1,0:T(8,128)S(1)}, f32[64,512]{1,0:T(8,128)S(1)}, u32[]{:S(2)}, u32[]{:S(2)}) collective-permute-start(f32[64,512]{1,0:T(8,128)S(1)} %add_add_fusion.1), channel_id=1, source_target_pairs={{0,4},{4,0},{8,12},{12,8},{16,20},{20,16},{24,28},{28,24},{1,5},{5... | collective-permute-start | bytes 393224 | tf_op jit(solution)/shard_map/ppermute | solution.py:173
  41.9 10.7 %collective-permute-start.17 = (f32[64,512]{1,0:T(8,128)S(1)}, f32[64,512]{1,0:T(8,128)S(1)}, u32[]{:S(2)}, u32[]{:S(2)}) collective-permute-start(f32[64,512]{1,0:T(8,128)S(1)} %copy-done.4), channel_id=1, source_target_pairs={{0,1},{1,0},{2,3},{3,2},{4,5},{5,4},{6,7},{7,6},{8,9},{9,8},{10,11... | collective-permute-start | bytes 393224 | tf_op jit(solution)/shard_map/ppermute | solution.py:173
  42.7 11.0 %collective-permute-start.18 = (f32[64,512]{1,0:T(8,128)S(1)}, f32[64,512]{1,0:T(8,128)S(1)}, u32[]{:S(2)}, u32[]{:S(2)}) collective-permute-start(f32[64,512]{1,0:T(8,128)S(1)} %copy-done.4), channel_id=1, source_target_pairs={{0,2},{1,3},{2,0},{3,1},{4,6},{5,7},{6,4},{7,5},{8,10},{9,11},{10,... | collective-permute-start | bytes 393224 | tf_op jit(solution)/shard_map/ppermute | solution.py:173
  43.8 16.5 %collective-permute-start.19 = (f32[64,512]{1,0:T(8,128)S(1)}, f32[64,512]{1,0:T(8,128)S(1)}, u32[]{:S(2)}, u32[]{:S(2)}) collective-permute-start(f32[64,512]{1,0:T(8,128)S(1)} %copy-done.4), channel_id=1, source_target_pairs={{0,3},{1,2},{2,1},{3,0},{4,7},{5,6},{6,5},{7,4},{8,11},{9,10},{10,... | collective-permute-start | bytes 393224 | tf_op jit(solution)/shard_map/ppermute | solution.py:173
  47.6 12.8 %collective-permute-start.14 = (f32[64,512]{1,0:T(8,128)S(1)}, f32[64,512]{1,0:T(8,128)S(1)}, u32[]{:S(2)}, u32[]{:S(2)}) collective-permute-start(f32[64,512]{1,0:T(8,128)S(1)} %add_add_fusion.2.refs_0_.agg), channel_id=1, source_target_pairs={{0,1},{1,0},{2,3},{3,2},{4,5},{5,4},{6,7},{7,6},{8,9},{9,8},{10,11... | collective-permute-start | bytes 393224 | tf_op jit(solution)/shard_map/ppermute | solution.py:173
  47.7 19.1 %collective-permute-start.15 = (f32[64,512]{1,0:T(8,128)S(1)}, f32[64,512]{1,0:T(8,128)S(1)}, u32[]{:S(2)}, u32[]{:S(2)}) collective-permute-start(f32[64,512]{1,0:T(8,128)S(1)} %add_add_fusion.2.refs_0_.agg), channel_id=1, source_target_pairs={{0,2},{1,3},{2,0},{3,1},{4,6},{5,7},{6,4},{7,5},{8,10},{9,11},{10,... | collective-permute-start | bytes 393224 | tf_op jit(solution)/shard_map/ppermute | solution.py:173
  52.6 18.5 %collective-permute-start.16 = (f32[64,512]{1,0:T(8,128)S(1)}, f32[64,512]{1,0:T(8,128)S(1)}, u32[]{:S(2)}, u32[]{:S(2)}) collective-permute-start(f32[64,512]{1,0:T(8,128)S(1)} %add_add_fusion.2.refs_0_.agg), channel_id=1, source_target_pairs={{0,3},{1,2},{2,1},{3,0},{4,7},{5,6},{6,5},{7,4},{8,11},{9,10},{10,... | collective-permute-start | bytes 393224 | tf_op jit(solution)/shard_map/ppermute | solution.py:173
  73.6 11.3 %collective-permute-start.20 = (f32[64,512]{1,0:T(8,128)S(1)}, f32[64,512]{1,0:T(8,128)S(1)}, u32[]{:S(2)}, u32[]{:S(2)}) collective-permute-start(f32[64,512]{1,0:T(8,128)S(1)} %get-tuple-element.31.refs_0_), channel_id=1, source_target_pairs={{0,4},{4,0},{8,12},{12,8},{16,20},{20,16},{24,28},{28,24},{1,5},{5... | collective-permute-start | bytes 393224 | tf_op jit(solution)/shard_map/ppermute | solution.py:173
  75.5 11.2 %collective-permute-start.21 = (f32[64,512]{1,0:T(8,128)S(1)}, f32[64,512]{1,0:T(8,128)S(1)}, u32[]{:S(2)}, u32[]{:S(2)}) collective-permute-start(f32[64,512]{1,0:T(8,128)S(1)} %get-tuple-element.31.refs_0_), channel_id=1, source_target_pairs={{0,24},{4,28},{8,0},{12,4},{16,8},{20,12},{24,16},{28,20},{1,25},{... | collective-permute-start | bytes 393224 | tf_op jit(solution)/shard_map/ppermute | solution.py:168
  76.7 8.6 %collective-permute-start.35 = (f32[64,256]{1,0:T(8,128)S(1)}, f32[64,256]{1,0:T(8,128)S(1)}, u32[]{:S(2)}, u32[]{:S(2)}) collective-permute-start(f32[64,256]{1,0:T(8,128)S(1)} %add.118), channel_id=1, source_target_pairs={{0,64},{32,96},{64,0},{96,32},{128,192},{160,224},{192,128},{224,1... | collective-permute-start | bytes 196616 | tf_op jit(solution)/shard_map/ppermute | solution.py:173
  76.8 11.9 %collective-permute-start.23 = (f32[64,512]{1,0:T(8,128)S(1)}, f32[64,512]{1,0:T(8,128)S(1)}, u32[]{:S(2)}, u32[]{:S(2)}) collective-permute-start(f32[64,512]{1,0:T(8,128)S(1)} %get-tuple-element.31.refs_0_), channel_id=1, source_target_pairs={{0,16},{4,20},{8,24},{12,28},{16,0},{20,4},{24,8},{28,12},{1,17},{... | collective-permute-start | bytes 393224 | tf_op jit(solution)/shard_map/ppermute | solution.py:168
  77.9 11.9 %collective-permute-start.25 = (f32[64,512]{1,0:T(8,128)S(1)}, f32[64,512]{1,0:T(8,128)S(1)}, u32[]{:S(2)}, u32[]{:S(2)}) collective-permute-start(f32[64,512]{1,0:T(8,128)S(1)} %get-tuple-element.31.refs_0_), channel_id=1, source_target_pairs={{0,8},{4,12},{8,16},{12,20},{16,24},{20,28},{24,0},{28,4},{1,9},{5... | collective-permute-start | bytes 393224 | tf_op jit(solution)/shard_map/ppermute | solution.py:168
  85.3 7.6 %collective-permute-start.24 = (f32[64,512]{1,0:T(8,128)S(1)}, f32[64,512]{1,0:T(8,128)S(1)}, u32[]{:S(2)}, u32[]{:S(2)}) collective-permute-start(f32[64,512]{1,0:T(8,128)S(1)} %collective-permute-done.20.refs_1_), channel_id=1, source_target_pairs={{0,16},{4,20},{8,24},{12,28},{16,0},{20,4},{24,8},{28,12},{1,17},{... | collective-permute-start | bytes 393224 | tf_op jit(solution)/shard_map/ppermute | solution.py:168
  88.7 15.0 %collective-permute-start.36 = (f32[64,256]{1,0:T(8,128)S(1)}, f32[64,256]{1,0:T(8,128)S(1)}, u32[]{:S(2)}, u32[]{:S(2)}) collective-permute-start(f32[64,256]{1,0:T(8,128)S(1)} %add.119), channel_id=1, source_target_pairs={{0,128},{32,160},{64,192},{96,224},{128,0},{160,32},{192,64},{224,... | collective-permute-start | bytes 196616 | tf_op jit(solution)/shard_map/ppermute | solution.py:173
  100.6 16.1 %collective-permute-start.28 = (f32[64,512]{1,0:T(8,128)S(1)}, f32[64,512]{1,0:T(8,128)S(1)}, u32[]{:S(2)}, u32[]{:S(2)}) collective-permute-start(f32[64,512]{1,0:T(8,128)S(1)} %get-tuple-element.35), channel_id=1, source_target_pairs={{0,32},{32,0},{64,96},{96,64},{128,160},{160,128},{192,224},{224,1... | collective-permute-start | bytes 393224 | tf_op jit(solution)/shard_map/ppermute | solution.py:173
  103.2 13.9 %collective-permute-start.30 = (f32[64,512]{1,0:T(8,128)S(1)}, f32[64,512]{1,0:T(8,128)S(1)}, u32[]{:S(2)}, u32[]{:S(2)}) collective-permute-start(f32[64,512]{1,0:T(8,128)S(1)} %get-tuple-element.37), channel_id=1, source_target_pairs={{0,32},{32,0},{64,96},{96,64},{128,160},{160,128},{192,224},{224,1... | collective-permute-start | bytes 393224 | tf_op jit(solution)/shard_map/ppermute | solution.py:173
  103.3 13.9 %collective-permute-start.32 = (f32[64,512]{1,0:T(8,128)S(1)}, f32[64,512]{1,0:T(8,128)S(1)}, u32[]{:S(2)}, u32[]{:S(2)}) collective-permute-start(f32[64,512]{1,0:T(8,128)S(1)} %get-tuple-element.39), channel_id=1, source_target_pairs={{0,32},{32,0},{64,96},{96,64},{128,160},{160,128},{192,224},{224,1... | collective-permute-start | bytes 393224 | tf_op jit(solution)/shard_map/ppermute | solution.py:173
  103.7 7.5 %collective-permute-start.37 = (f32[64,256]{1,0:T(8,128)S(1)}, f32[64,256]{1,0:T(8,128)S(1)}, u32[]{:S(2)}, u32[]{:S(2)}) collective-permute-start(f32[64,256]{1,0:T(8,128)S(1)} %add.120), channel_id=1, source_target_pairs={{0,4},{4,0},{8,12},{12,8},{16,20},{20,16},{24,28},{28,24},{1,5},{5... | collective-permute-start | bytes 196616 | tf_op jit(solution)/shard_map/ppermute | solution.py:173
  111.3 8.7 %collective-permute-start.38 = (f32[64,256]{1,0:T(8,128)S(1)}, f32[64,256]{1,0:T(8,128)S(1)}, u32[]{:S(2)}, u32[]{:S(2)}) collective-permute-start(f32[64,256]{1,0:T(8,128)S(1)} %add.121), channel_id=1, source_target_pairs={{0,8},{4,12},{8,0},{12,4},{16,24},{20,28},{24,16},{28,20},{1,9},{5... | collective-permute-start | bytes 196616 | tf_op jit(solution)/shard_map/ppermute | solution.py:173
  115.5 10.1 %collective-permute-start.27 = (f32[64,512]{1,0:T(8,128)S(1)}, f32[64,512]{1,0:T(8,128)S(1)}, u32[]{:S(2)}, u32[]{:S(2)}) collective-permute-start(f32[64,512]{1,0:T(8,128)S(1)} %get-tuple-element.33), channel_id=1, source_target_pairs={{0,32},{32,0},{64,96},{96,64},{128,160},{160,128},{192,224},{224,1... | collective-permute-start | bytes 393224 | tf_op jit(solution)/shard_map/ppermute | solution.py:173
  116.8 8.9 %collective-permute-start.29 = (f32[64,512]{1,0:T(8,128)S(1)}, f32[64,512]{1,0:T(8,128)S(1)}, u32[]{:S(2)}, u32[]{:S(2)}) collective-permute-start(f32[64,512]{1,0:T(8,128)S(1)} %add.112), channel_id=1, source_target_pairs={{0,128},{32,160},{64,192},{96,224},{128,0},{160,32},{192,64},{224,... | collective-permute-start | bytes 393224 | tf_op jit(solution)/shard_map/ppermute | solution.py:168
  117.1 9.4 %collective-permute-start.31 = (f32[64,512]{1,0:T(8,128)S(1)}, f32[64,512]{1,0:T(8,128)S(1)}, u32[]{:S(2)}, u32[]{:S(2)}) collective-permute-start(f32[64,512]{1,0:T(8,128)S(1)} %add.114), channel_id=1, source_target_pairs={{0,64},{32,96},{64,128},{96,160},{128,192},{160,224},{192,0},{224,... | collective-permute-start | bytes 393224 | tf_op jit(solution)/shard_map/ppermute | solution.py:168
  117.3 9.2 %collective-permute-start.33 = (f32[64,512]{1,0:T(8,128)S(1)}, f32[64,512]{1,0:T(8,128)S(1)}, u32[]{:S(2)}, u32[]{:S(2)}) collective-permute-start(f32[64,512]{1,0:T(8,128)S(1)} %add.116), channel_id=1, source_target_pairs={{0,192},{32,224},{64,0},{96,32},{128,64},{160,96},{192,128},{224,1... | collective-permute-start | bytes 393224 | tf_op jit(solution)/shard_map/ppermute | solution.py:168
  (13 other events, 104.9 us)

commit v2 on v0

v2 whole, which is shorter than its diff:
```python
import functools
import math

import jax
import jax.numpy as jnp
from jax import lax
from jax.experimental import pallas as pl
from jax.experimental.pallas import tpu as pltpu
from jax.sharding import PartitionSpec as P


BF16 = jnp.bfloat16
F32 = jnp.float32
NT = (((1,), (1,)), ((), ()))
NN = (((1,), (0,)), ((), ()))
GROUP = 16
RING = 4
ROOT_2_PI = 0.7978845608028654
CUBIC = 0.044715
SMALL = 16 << 20

dot = functools.partial(lax.dot_general, preferred_element_type=F32)


def split(x):
    high = x.astype(BF16)
    return high, (x - high.astype(F32)).astype(BF16)


def dot3(a, b, dims):
    a_high, a_low = split(a)
    b_high, b_low = split(b)
    return dot(a_high, b_high, dims) + dot(a_high, b_low, dims) + dot(a_low, b_high, dims)


def spmm_kernel(transposed, n_in, n_out, table, *refs):
    sources = refs[:n_in]
    values = refs[n_in]
    outs = refs[n_in + 1 : n_in + 1 + n_out]
    buf, sem, held, acc = refs[n_in + 1 + n_out :]
    edge = values.shape[-1]
    width = acc.shape[1]
    to_row, from_row = (2, 3) if transposed else (0, 1)
    groups = (table[5, 0] + GROUP - 1) // GROUP

    def copy(group, u):
        slot = lax.rem(group, RING)
        return pltpu.make_async_copy(
            values.at[table[4, group * GROUP + u]], buf.at[slot, u], sem.at[slot, u]
        )

    def start(group):
        def one(u, carry):
            copy(group, u).start()
            return carry

        lax.fori_loop(0, GROUP, one, 0, unroll=4)

    for g in range(RING - 1):

        @pl.when(g < groups)
        def _():
            start(g)

    per = held.shape[0] // n_in
    for b in range(n_in):
        for j in range(per):
            ref = sources[b]
            tile = ref[:, j * edge : (j + 1) * edge] if ref.ndim == 2 else ref[j]
            high, low = split(tile)
            held[b * per + j, :width] = high
            held[b * per + j, width:] = low
    acc[...] = jnp.zeros_like(acc)

    def step(group, carry):
        @pl.when(group + RING - 1 < groups)
        def _():
            start(group + RING - 1)

        for u in range(GROUP):
            copy(group, u).wait()
        slot = lax.rem(group, RING)
        products = []
        for u in range(GROUP):
            both = held[table[from_row, group * GROUP + u]]
            high, low = split(buf[slot, u])
            if transposed:
                p = dot(both, high, NN)
                products.append(p[:width] + p[width:] + dot(both[:width], low, NN))
            else:
                p = dot(both, jnp.concatenate([high, low], 0), NT)
                products.append(p[:width, :edge] + p[:width, edge:] + p[width:, :edge])
        for u in range(GROUP):
            to = table[to_row, group * GROUP + u]
            acc[to] = acc[to] + products[u]
        return carry

    lax.fori_loop(0, groups, step, 0)
    per = acc.shape[0] // n_out
    for b in range(n_out):
        for j in range(per):
            if outs[b].ndim == 2:
                outs[b][:, j * edge : (j + 1) * edge] = acc[b * per + j]
            else:
                outs[b][j] = acc[b * per + j]


def spmm(table, sources, values, n_from, n_out, out_shape, width, transposed):
    n_in = len(sources)
    slots, edge, _ = values.shape
    n_to = n_out * math.prod(out_shape) // (width * edge)
    vmem = pl.BlockSpec(memory_space=pltpu.VMEM)
    return pl.pallas_call(
        functools.partial(spmm_kernel, transposed, n_in, n_out),
        in_specs=[pl.BlockSpec(memory_space=pltpu.SMEM)]
        + [vmem] * n_in
        + [pl.BlockSpec(memory_space=pl.ANY)],
        out_specs=[vmem] * n_out,
        out_shape=[jax.ShapeDtypeStruct(out_shape, F32)] * n_out,
        scratch_shapes=[
            pltpu.VMEM((RING, GROUP, edge, edge), F32),
            pltpu.SemaphoreType.DMA((RING, GROUP)),
            pltpu.VMEM((n_from, 2 * width, edge), BF16),
            pltpu.VMEM((n_to + 1, width, edge), F32),
        ],
        compiler_params=pltpu.CompilerParams(vmem_limit_bytes=51 << 20),
        cost_estimate=pl.CostEstimate(
            flops=6 * slots * width * edge * edge, bytes_accessed=14 << 20, transcendentals=0
        ),
        name="spmm_back" if transposed else "spmm",
    )(table, *sources, values)


def small(body, out_shapes, *args, scalars=1, scratch=(), flops=1 << 20):
    vmem = pl.BlockSpec(memory_space=pltpu.VMEM)
    call = pl.pallas_call(
        body,
        in_specs=[pl.BlockSpec(memory_space=pltpu.SMEM)] * scalars
        + [vmem] * (len(args) - scalars),
        out_specs=[vmem] * len(out_shapes),
        out_shape=[jax.ShapeDtypeStruct(shape, F32) for shape in out_shapes],
        scratch_shapes=[pltpu.VMEM(shape, F32) for shape in scratch],
        compiler_params=pltpu.CompilerParams(vmem_limit_bytes=SMALL),
        cost_estimate=pl.CostEstimate(flops=flops, bytes_accessed=1 << 20, transcendentals=0),
    )
    return list(call(*args))


def part(n, size, index):
    return pl.ds(pl.multiple_of(lax.rem(index + 2 * n, n) * size, size), size)


def cut_kernel(place, whole, *outs):
    n = len(outs)
    size = whole.shape[1] // n
    for d in range(n):
        outs[d][...] = whole[:, part(n, size, place[0] + d)]


def join_kernel(place, *refs):
    out = refs[-1]
    n = len(refs) - 1
    size = out.shape[1] // n
    for d in range(n):
        out[:, part(n, size, place[0] - d)] = refs[d][...]


def fold_kernel(n, *refs):
    for i in range(refs[0].shape[0]):
        total = refs[0][i]
        for k in range(1, n):
            total = total + refs[k][i]
        refs[n + i][...] = total


def stack_kernel(*refs):
    out = refs[-1]
    n = len(refs) - 1
    for i in range(n):
        out[i] = refs[i][0]
    for j in range(1, refs[0].shape[0]):
        total = refs[0][j]
        for i in range(1, n):
            total = total + refs[i][j]
        out[n + j - 1] = total


def tail_kernel(first, *refs):
    out = refs[-1]
    for j in range(out.shape[0]):
        total = refs[0][first + j]
        for ref in refs[1:-1]:
            total = total + ref[first + j]
        out[j] = total


def mid_kernel(n_rep, n_z, scale, place, *refs):
    sums = refs[:n_z]
    cots = refs[n_z : n_z + n_rep]
    weight, weight_t = refs[n_z + n_rep : n_z + n_rep + 2]
    refs = refs[n_z + n_rep + 2 :]
    grads = refs[:n_rep]
    acts = refs[n_rep : 2 * n_rep]
    agg, cot, act, mixed_grad, weight_grad = refs[2 * n_rep :]
    quarter, edge = sums[0].shape
    me = place[0]
    for d in range(n_rep):
        total = sums[d][...]
        for e in range(d + n_rep, n_z, n_rep):
            total = total + sums[e][...]
        agg[part(n_rep, quarter, me - d), :] = total
        cot[part(n_rep, quarter, me - d), :] = cots[d][...]
    pre = dot3(weight_t[...], agg[...], NN)
    square = pre * pre
    curve = jnp.tanh(ROOT_2_PI * (pre + CUBIC * (square * pre)))
    half = 0.5 * (1.0 + curve)
    act[...] = pre * half
    slope = half + 0.5 * pre * (1.0 - curve * curve) * (
        ROOT_2_PI * (1.0 + 3.0 * CUBIC * square)
    )
    grad = cot[...] * slope
    mixed_grad[...] = dot3(weight[...], grad, NN)
    weight_grad[...] = dot3(agg[...], grad, NT) * scale
    for d in range(n_rep):
        at = part(n_rep, quarter, me + d)
        grads[d][0] = mixed_grad[at, :]
        for j in range(1, grads[d].shape[0]):
            grads[d][j] = weight_grad[at, (j - 1) * edge : j * edge]
        acts[d][...] = act[at, :]


def shift(x, axis, by):
    n = lax.axis_size(axis)
    return lax.ppermute(x, axis, [(i, (i + by) % n) for i in range(n)])


def shift_z(x, by):
    n = lax.axis_size(("col", "rep"))
    m = 2 * lax.axis_size("rep")
    return lax.ppermute(x, ("col", "rep"), [(i, i // m * m + (i + by) % m) for i in range(n)])


def swap(x, axis, bit):
    n = lax.axis_size(axis)
    return lax.ppermute(x, axis, [(i, i ^ bit) for i in range(n)])


def layer(features, weight, cotangent, tile_values, tile_row, tile_col, tile_kind, tile_count):
    n_row, n_col, n_rep = (lax.axis_size(a) for a in ("row", "col", "rep"))
    row, col, rep = (lax.axis_index(a) for a in ("row", "col", "rep"))
    n_x, n_y, n_z = n_col // 2, n_row // 2, 2 * n_rep
    width, stretch = features.shape
    edge = tile_values.shape[1]
    per = stretch // edge
    slots = tile_kind.shape[0]
    full = weight.shape[0]
    z = (col & 1) * n_rep + rep
    place = rep.astype(jnp.int32)[None]

    far_x = ((tile_row // n_z - col // 2) & (n_x - 1)) * n_z
    at_z = tile_row & (n_z - 1)
    stretch_of = tile_col // per
    far_y = (stretch_of // 2 - row // 2) & (n_y - 1)
    by_col = (far_y * 2 + ((stretch_of ^ row) & 1)) * per + (tile_col & (per - 1))
    live = jnp.arange(slots, dtype=jnp.int32) < tile_count[0]
    table = jnp.stack(
        [
            jnp.where(live, far_x + ((at_z - z) & (n_z - 1)), n_x * n_z),
            by_col,
            jnp.where(live, by_col, n_row * per),
            far_x + ((z - at_z) & (n_z - 1)),
            tile_kind,
            jnp.broadcast_to(tile_count, (slots,)),
        ]
    )
    blocks = []
    for k in range(n_y):
        x = shift(features, "row", -2 * k) if k else features
        blocks += [x, swap(x, "row", 1)]
    pieces = small(cut_kernel, [(width, edge)] * n_rep, place, cotangent)
    cots = pieces[:1]
    for d in range(1, n_rep):
        cots.append(shift(pieces[d], "rep", d))
    parts = spmm(
        table, blocks, tile_values, n_row * per, n_x, (n_z, width, edge), width, False
    )
    got = [parts[0]] + [shift(parts[k], "col", 2 * k) for k in range(1, n_x)]
    sums = small(
        functools.partial(fold_kernel, n_x),
        [(width, edge)] * n_z, *got, scalars=0,
    )
    for d in range(1, n_z):
        sums[d] = shift_z(sums[d], d)
    scale = float(stretch * n_row * n_col) ** (-0.5)
    extra = full // edge
    outs = small(
        functools.partial(mid_kernel, n_rep, n_z, scale),
        [(1 + extra, width, edge)] * n_rep + [(width, edge)] * n_rep,
        place, *sums, *cots, weight, weight.T,
        scratch=[(full, edge)] * 4 + [(full, full)], flops=18 * full * full * edge,
    )
    grads, acts = outs[:n_rep], outs[n_rep:]
    pieces = grads[:1]
    for d in range(1, n_z):
        pieces.append(shift_z(grads[d % n_rep], d))
    blocks = small(stack_kernel, [(n_z + extra, width, edge)], *pieces, scalars=0)
    for k in range(1, n_x):
        blocks.append(shift(blocks[0], "col", -2 * k))
    (weight_grad,) = small(
        functools.partial(tail_kernel, n_z),
        [(extra, width, edge)], *blocks, scalars=0,
    )

    def add_swapped(x, axis, bit):
        return x + swap(x, axis, bit)

    weight_grad = add_swapped(weight_grad, "row", 1)
    for d in range(1, n_rep):
        acts[d] = shift(acts[d], "rep", d)
    (output,) = small(join_kernel, [(width, stretch)], place, *acts)
    parts = spmm(
        table, blocks, tile_values, n_x * n_z, n_row, (width, stretch), width, True
    )
    totals = [parts[2 * k] + swap(parts[2 * k + 1], "row", 1) for k in range(n_y)]
    input_grad = totals[0]
    for k in (2, 1, 3):
        got = shift(totals[k], "row", 2 * k)
        input_grad = input_grad + got
    weight_grad = add_swapped(weight_grad, "row", 2)
    weight_grad = add_swapped(weight_grad, "row", 4)
    weight_grad = jnp.concatenate([weight_grad[j] for j in range(extra)], axis=1)
    return (output, input_grad, weight_grad)


def solution(mesh):
    return jax.shard_map(
        layer,
        mesh=mesh,
        in_specs=(
            P("rep", ("col", "row")),
            P(),
            P("rep", ("row", "col")),
            P(("row", "col"), None, None),
            P(("row", "col")),
            P(("row", "col")),
            P(("row", "col")),
            P(("row", "col")),
        ),
        out_specs=(P("rep", ("row", "col")), P("rep", ("col", "row")), P("rep", None)),
        check_vma=False,
    )
```

time: 119 us -> 137 us (1.15); the launches traced: 117 us -> 136 us
  waiting for transfers between devices: 23 us -> 45.4 us
  starting transfers between devices: 75.1 us -> 71.1 us
    ppermute x22 -> x11, starting transfers between devices: 41.1 us -> 6.16 us  [swap(): return lax.ppermute(x, axis, [(i, i ^ bit) for i in range(n)])]
    ppermute x0 -> x14, starting transfers between devices: none -> 33.4 us  [shift_z(): lax.ppermute(x, ('col', 'rep'), [(i, i // m * m + (i + by) % m) for i in...]
    ppermute x18, waiting for transfers between devices: 4.12 us -> 32 us  [shift(): return lax.ppermute(x, axis, [(i, (i + by) % n) for i in range(n)])]
    ppermute x22 -> x11, waiting for transfers between devices: 18.9 us -> 1.27 us  [swap(): return lax.ppermute(x, axis, [(i, i ^ bit) for i in range(n)])]
    ppermute x0 -> x14, waiting for transfers between devices: none -> 12.2 us  [shift_z(): lax.ppermute(x, ('col', 'rep'), [(i, i // m * m + (i + by) % m) for i in...]
    ppermute x18, starting transfers between devices: 34 us -> 31.6 us  [shift(): return lax.ppermute(x, axis, [(i, (i + by) % n) for i in range(n)])]
  transfers between devices with their start and end apart: 40 -> 43, of which waited for: 10 -> 18; matrix products, arithmetic and copies ran while one was open for 2% -> 3% of each run, Pallas kernels for 5% -> 5%
where the time goes in v2:
time: 137 us; the launch traced here: 136 us
  starting transfers between devices  71.1 us (52%)
  waiting for transfers between devices  45.4 us (33%)
  Pallas kernels  13 us (9%)
  other arithmetic  3.5 us (3%)
  local copies, waits for them, and re-layouts  1.75 us (1%)
  between operations  1.51 us (1%)
    ppermute x14, starting transfers between devices, shift_z(): lax.ppermute(x, ('col', 'rep'), [(i, i // m * m + (i + by) % m) for i in...  33.4 us
    ppermute x18, waiting for transfers between devices, shift(): return lax.ppermute(x, axis, [(i, (i + by) % n) for i in range(n)])  32 us
    ppermute x18, starting transfers between devices, shift(): return lax.ppermute(x, axis, [(i, (i + by) % n) for i in range(n)])  31.6 us
    ppermute x14, waiting for transfers between devices, shift_z(): lax.ppermute(x, ('col', 'rep'), [(i, i // m * m + (i + by) % m) for i in...  12.2 us
    pallas_call x2, Pallas kernels, spmm(): pl.pallas_call(functools.partial(spmm_kernel, transposed, n_in, n_out), i...  11.4 us
    ppermute x11, starting transfers between devices, swap(): return lax.ppermute(x, axis, [(i, i ^ bit) for i in range(n)])  6.16 us
  transfers between devices with their start and end apart: 43, of which 18 were waited for; matrix products, arithmetic and copies ran while one was open for 3% of the time, Pallas kernels for 5%

profile of v2, /device:TPU:2, one launch (start us, length us, event | category | flops | bytes accessed | tf_op | source)
XLA Modules:
  0.0 136.2 jit_solution(3629949565166950170)
XLA Ops:
  0.6 3.3 %collective-permute-start.3 = (f32[64,512]{1,0:T(8,128)}, f32[64,512]{1,0:T(8,128)S(1)}, u32[]{:S(2)}, u32[]{:S(2)}) collective-permute-start(f32[64,512]{1,0:T(8,128)} %refs_0_.1), channel_id=1, source_target_pairs={{0,128},{32,160},{64,192},{96,224},{128,0},{160,32},{192,64},{224,... | collective-permute-start | bytes 393224 | tf_op jit(solution)/shard_map/ppermute | solution.py:234
  8.2 2.6 %collective-permute-done.1.refs_2_ = f32[64,512]{1,0:T(8,128)S(1)} collective-permute-done((f32[64,512]{1,0:T(8,128)}, f32[64,512]{1,0:T(8,128)S(1)}, u32[]{:S(2)}, u32[]{:S(2)}) %collective-permute-start.1) | collective-permute-done | bytes 131104 | tf_op jit(solution)/shard_map/ppermute | solution.py:234
  14.7 5.7 %spmm.1 = (f32[8,64,128]{2,1,0:T(8,128)S(1)}, f32[8,64,128]{2,1,0:T(8,128)S(1)}, f32[8,64,128]{2,1,0:T(8,128)S(1)}, f32[8,64,128]{2,1,0:T(8,128)S(1)}) custom-call(s32[6,160]{1,0:T(8,128)S(1)} %stack.23.table, f32[64,512]{1,0:T(8,128)S(1)} %copy-done.1, f32[64,512]{1,0:T(8,128)S(1)} %collective-permute-done.refs_1_, ...), custom_call_target="tpu_custom_call" | custom-call | flops 1006632960 | bytes 14680064 | tf_op jit(solution)/shard_map/spmm/pallas_call | solution.py:113
  20.4 2.7 %collective-permute-start.7 = (f32[8,64,128]{2,1,0:T(8,128)S(1)}, f32[8,64,128]{2,1,0:T(8,128)S(1)}, u32[]{:S(2)}, u32[]{:S(2)}) collective-permute-start(f32[8,64,128]{2,1,0:T(8,128)S(1)} %get-tuple-element.36), channel_id=1, source_target_pairs={{0,8},{4,12},{8,16},{12,20},{16,24},{20,28},{24,0},{28,4},{1,9},{5... | collective-permute-start | bytes 786440 | tf_op jit(solution)/shard_map/ppermute | solution.py:234
  23.1 2.3 %collective-permute-start.8 = (f32[8,64,128]{2,1,0:T(8,128)S(1)}, f32[8,64,128]{2,1,0:T(8,128)S(1)}, u32[]{:S(2)}, u32[]{:S(2)}) collective-permute-start(f32[8,64,128]{2,1,0:T(8,128)S(1)} %get-tuple-element.37), channel_id=1, source_target_pairs={{0,16},{4,20},{8,24},{12,28},{16,0},{20,4},{24,8},{28,12},{1,17},{... | collective-permute-start | bytes 786440 | tf_op jit(solution)/shard_map/ppermute | solution.py:234
  25.4 2.0 %collective-permute-start.17 = (f32[64,128]{1,0:T(8,128)S(1)}, f32[64,128]{1,0:T(8,128)S(1)}, u32[]{:S(2)}, u32[]{:S(2)}) collective-permute-start(f32[64,128]{1,0:T(8,128)S(1)} %get-tuple-element.48), channel_id=1, source_target_pairs={{0,1},{1,2},{2,3},{3,0},{4,5},{5,6},{6,7},{7,4},{8,9},{9,10},{10,1... | collective-permute-start | bytes 98312 | tf_op jit(solution)/shard_map/ppermute | solution.py:234
  27.4 3.3 %collective-permute-start.18 = (f32[64,128]{1,0:T(8,128)S(1)}, f32[64,128]{1,0:T(8,128)S(1)}, u32[]{:S(2)}, u32[]{:S(2)}) collective-permute-start(f32[64,128]{1,0:T(8,128)S(1)} %get-tuple-element.49), channel_id=1, source_target_pairs={{0,2},{1,3},{2,0},{3,1},{4,6},{5,7},{6,4},{7,5},{8,10},{9,11},{10,... | collective-permute-start | bytes 98312 | tf_op jit(solution)/shard_map/ppermute | solution.py:234
  30.7 4.4 %collective-permute-start.19 = (f32[64,128]{1,0:T(8,128)S(1)}, f32[64,128]{1,0:T(8,128)S(1)}, u32[]{:S(2)}, u32[]{:S(2)}) collective-permute-start(f32[64,128]{1,0:T(8,128)S(1)} %get-tuple-element.50), channel_id=1, source_target_pairs={{0,3},{1,0},{2,1},{3,2},{4,7},{5,4},{6,5},{7,6},{8,11},{9,8},{10,9... | collective-permute-start | bytes 98312 | tf_op jit(solution)/shard_map/ppermute | solution.py:234
  35.1 2.7 %collective-permute-done.9.refs_3_ = f32[8,64,128]{2,1,0:T(8,128)S(1)} collective-permute-done((f32[8,64,128]{2,1,0:T(8,128)S(1)}, f32[8,64,128]{2,1,0:T(8,128)S(1)}, u32[]{:S(2)}, u32[]{:S(2)}) %collective-permute-start.9) | collective-permute-done | bytes 262176 | tf_op jit(solution)/shard_map/ppermute | solution.py:234
  37.9 2.0 %collective-permute-start.10 = (f32[64,128]{1,0:T(8,128)S(1)}, f32[64,128]{1,0:T(8,128)S(1)}, u32[]{:S(2)}, u32[]{:S(2)}) collective-permute-start(f32[64,128]{1,0:T(8,128)S(1)} %get-tuple-element.40), channel_id=1, source_target_pairs={{0,1},{1,2},{2,3},{3,4},{4,5},{5,6},{6,7},{7,0},{8,9},{9,10},{10,1... | collective-permute-start | bytes 98312 | tf_op jit(solution)/shard_map/ppermute | solution.py:240
  39.9 3.3 %collective-permute-start.11 = (f32[64,128]{1,0:T(8,128)S(1)}, f32[64,128]{1,0:T(8,128)S(1)}, u32[]{:S(2)}, u32[]{:S(2)}) collective-permute-start(f32[64,128]{1,0:T(8,128)S(1)} %get-tuple-element.41), channel_id=1, source_target_pairs={{0,2},{1,3},{2,4},{3,5},{4,6},{5,7},{6,0},{7,1},{8,10},{9,11},{10,... | collective-permute-start | bytes 98312 | tf_op jit(solution)/shard_map/ppermute | solution.py:240
  43.2 3.7 %collective-permute-start.12 = (f32[64,128]{1,0:T(8,128)S(1)}, f32[64,128]{1,0:T(8,128)S(1)}, u32[]{:S(2)}, u32[]{:S(2)}) collective-permute-start(f32[64,128]{1,0:T(8,128)S(1)} %get-tuple-element.42), channel_id=1, source_target_pairs={{0,3},{1,4},{2,5},{3,6},{4,7},{5,0},{6,1},{7,2},{8,11},{9,12},{10,... | collective-permute-start | bytes 98312 | tf_op jit(solution)/shard_map/ppermute | solution.py:240
  47.7 4.6 %collective-permute-start.14 = (f32[64,128]{1,0:T(8,128)S(1)}, f32[64,128]{1,0:T(8,128)S(1)}, u32[]{:S(2)}, u32[]{:S(2)}) collective-permute-start(f32[64,128]{1,0:T(8,128)S(1)} %get-tuple-element.44), channel_id=1, source_target_pairs={{0,5},{1,6},{2,7},{3,0},{4,1},{5,2},{6,3},{7,4},{8,13},{9,14},{10,... | collective-permute-start | bytes 98312 | tf_op jit(solution)/shard_map/ppermute | solution.py:240
  52.4 2.7 %collective-permute-start.15 = (f32[64,128]{1,0:T(8,128)S(1)}, f32[64,128]{1,0:T(8,128)S(1)}, u32[]{:S(2)}, u32[]{:S(2)}) collective-permute-start(f32[64,128]{1,0:T(8,128)S(1)} %get-tuple-element.45), channel_id=1, source_target_pairs={{0,6},{1,7},{2,0},{3,1},{4,2},{5,3},{6,4},{7,5},{8,14},{9,15},{10,... | collective-permute-start | bytes 98312 | tf_op jit(solution)/shard_map/ppermute | solution.py:240
  61.4 2.8 %collective-permute-start.27 = (f32[3,64,128]{2,1,0:T(8,128)S(1)}, f32[3,64,128]{2,1,0:T(8,128)S(1)}, u32[]{:S(2)}, u32[]{:S(2)}) collective-permute-start(f32[3,64,128]{2,1,0:T(8,128)S(1)} %get-tuple-element.56), channel_id=1, source_target_pairs={{0,5},{1,6},{2,7},{3,0},{4,1},{5,2},{6,3},{7,4},{8,13},{9,14},{10,... | collective-permute-start | bytes 294920 | tf_op jit(solution)/shard_map/ppermute | solution.py:240
  65.2 2.8 %collective-permute-start.28 = (f32[3,64,128]{2,1,0:T(8,128)S(1)}, f32[3,64,128]{2,1,0:T(8,128)S(1)}, u32[]{:S(2)}, u32[]{:S(2)}) collective-permute-start(f32[3,64,128]{2,1,0:T(8,128)S(1)} %get-tuple-element.57), channel_id=1, source_target_pairs={{0,6},{1,7},{2,0},{3,1},{4,2},{5,3},{6,4},{7,5},{8,14},{9,15},{10,... | collective-permute-start | bytes 294920 | tf_op jit(solution)/shard_map/ppermute | solution.py:240
  69.2 5.1 %collective-permute-start.29 = (f32[3,64,128]{2,1,0:T(8,128)S(1)}, f32[3,64,128]{2,1,0:T(8,128)S(1)}, u32[]{:S(2)}, u32[]{:S(2)}) collective-permute-start(f32[3,64,128]{2,1,0:T(8,128)S(1)} %get-tuple-element.58), channel_id=1, source_target_pairs={{0,7},{1,0},{2,1},{3,2},{4,3},{5,4},{6,5},{7,6},{8,15},{9,8},{10,9... | collective-permute-start | bytes 294920 | tf_op jit(solution)/shard_map/ppermute | solution.py:240
  74.3 2.4 %collective-permute-done.27.refs_5_ = f32[3,64,128]{2,1,0:T(8,128)S(1)} collective-permute-done((f32[3,64,128]{2,1,0:T(8,128)S(1)}, f32[3,64,128]{2,1,0:T(8,128)S(1)}, u32[]{:S(2)}, u32[]{:S(2)}) %collective-permute-start.27) | collective-permute-done | bytes 98336 | tf_op jit(solution)/shard_map/ppermute | solution.py:240
  76.7 1.7 %collective-permute-start.25 = (f32[3,64,128]{2,1,0:T(8,128)S(1)}, f32[3,64,128]{2,1,0:T(8,128)S(1)}, u32[]{:S(2)}, u32[]{:S(2)}) collective-permute-start(f32[3,64,128]{2,1,0:T(8,128)S(1)} %get-tuple-element.58), channel_id=1, source_target_pairs={{0,3},{1,4},{2,5},{3,6},{4,7},{5,0},{6,1},{7,2},{8,11},{9,12},{10,... | collective-permute-start | bytes 294920 | tf_op jit(solution)/shard_map/ppermute | solution.py:240
  80.0 4.4 %collective-permute-done.25.refs_3_ = f32[3,64,128]{2,1,0:T(8,128)S(1)} collective-permute-done((f32[3,64,128]{2,1,0:T(8,128)S(1)}, f32[3,64,128]{2,1,0:T(8,128)S(1)}, u32[]{:S(2)}, u32[]{:S(2)}) %collective-permute-start.25) | collective-permute-done | bytes 98336 | tf_op jit(solution)/shard_map/ppermute | solution.py:240
  85.3 4.1 %collective-permute-start.31 = (f32[10,64,128]{2,1,0:T(8,128)S(1)}, f32[10,64,128]{2,1,0:T(8,128)S(1)}, u32[]{:S(2)}, u32[]{:S(2)}) collective-permute-start(f32[10,64,128]{2,1,0:T(8,128)S(1)} %shard_map.107.refs_0_), channel_id=1, source_target_pairs={{0,16},{4,20},{8,24},{12,28},{16,0},{20,4},{24,8},{28,12},{1,17},{... | collective-permute-start | bytes 983048 | tf_op jit(solution)/shard_map/ppermute | solution.py:234
  90.2 5.1 %collective-permute-done.32.refs_3_ = f32[10,64,128]{2,1,0:T(8,128)S(1)} collective-permute-done((f32[10,64,128]{2,1,0:T(8,128)S(1)}, f32[10,64,128]{2,1,0:T(8,128)S(1)}, u32[]{:S(2)}, u32[]{:S(2)}) %collective-permute-start.32) | collective-permute-done | bytes 327712 | tf_op jit(solution)/shard_map/ppermute | solution.py:234
  95.3 2.7 %collective-permute-done.31.refs_2_ = f32[10,64,128]{2,1,0:T(8,128)S(1)} collective-permute-done((f32[10,64,128]{2,1,0:T(8,128)S(1)}, f32[10,64,128]{2,1,0:T(8,128)S(1)}, u32[]{:S(2)}, u32[]{:S(2)}) %collective-permute-start.31) | collective-permute-done | bytes 327712 | tf_op jit(solution)/shard_map/ppermute | solution.py:234
  98.0 3.6 %collective-permute-done.30.refs_1_ = f32[10,64,128]{2,1,0:T(8,128)S(1)} collective-permute-done((f32[10,64,128]{2,1,0:T(8,128)S(1)}, f32[10,64,128]{2,1,0:T(8,128)S(1)}, u32[]{:S(2)}, u32[]{:S(2)}) %collective-permute-start.30) | collective-permute-done | bytes 327712 | tf_op jit(solution)/shard_map/ppermute | solution.py:234
  103.1 5.7 %spmm_back.1 = (f32[64,512]{1,0:T(8,128)S(1)}, f32[64,512]{1,0:T(8,128)S(1)}, f32[64,512]{1,0:T(8,128)S(1)}, f32[64,512]{1,0:T(8,128)S(1)}, f32[64,512]{1,0:T(8,...) custom-call(s32[6,160]{1,0:T(8,128)S(1)} %stack.23.table, ...), custom_call_target="tpu_custom_call" | custom-call | flops 1006632960 | bytes 14680064 | tf_op jit(solution)/shard_map/spmm_back/pallas_call | solution.py:113
  109.6 1.7 %collective-permute-start.21 = (f32[64,128]{1,0:T(8,128)S(1)}, f32[64,128]{1,0:T(8,128)S(1)}, u32[]{:S(2)}, u32[]{:S(2)}) collective-permute-start(f32[64,128]{1,0:T(8,128)S(1)} %get-tuple-element.53), channel_id=1, source_target_pairs={{0,2},{1,3},{2,0},{3,1},{4,6},{5,7},{6,4},{7,5},{8,10},{9,11},{10,... | collective-permute-start | bytes 98312 | tf_op jit(solution)/shard_map/ppermute | solution.py:234
  111.3 4.3 %collective-permute-done.20.refs_1_ = f32[64,128]{1,0:T(8,128)S(1)} collective-permute-done((f32[64,128]{1,0:T(8,128)S(1)}, f32[64,128]{1,0:T(8,128)S(1)}, u32[]{:S(2)}, u32[]{:S(2)}) %collective-permute-start.20) | collective-permute-done | bytes 32800 | tf_op jit(solution)/shard_map/ppermute | solution.py:234
  115.6 5.0 %collective-permute-start.42 = (f32[2,64,128]{2,1,0:T(8,128)S(1)}, f32[2,64,128]{2,1,0:T(8,128)S(1)}, u32[]{:S(2)}, u32[]{:S(2)}) collective-permute-start(f32[2,64,128]{2,1,0:T(8,128)S(1)} %add.63), channel_id=1, source_target_pairs={{0,128},{32,160},{64,192},{96,224},{128,0},{160,32},{192,64},{224,... | collective-permute-start | bytes 196616 | tf_op jit(solution)/shard_map/ppermute | solution.py:245
  120.6 3.9 %collective-permute-done.22.refs_3_ = f32[64,128]{1,0:T(8,128)S(1)} collective-permute-done((f32[64,128]{1,0:T(8,128)S(1)}, f32[64,128]{1,0:T(8,128)S(1)}, u32[]{:S(2)}, u32[]{:S(2)}) %collective-permute-start.22) | collective-permute-done | bytes 32800 | tf_op jit(solution)/shard_map/ppermute | solution.py:234
  125.9 2.2 %collective-permute-start.37 = (f32[64,512]{1,0:T(8,128)S(1)}, f32[64,512]{1,0:T(8,128)S(1)}, u32[]{:S(2)}, u32[]{:S(2)}) collective-permute-start(f32[64,512]{1,0:T(8,128)S(1)} %add.58), channel_id=1, source_target_pairs={{0,64},{32,96},{64,128},{96,160},{128,192},{160,224},{192,0},{224,... | collective-permute-start | bytes 393224 | tf_op jit(solution)/shard_map/ppermute | solution.py:234
  130.0 3.2 %collective-permute-done.35 = f32[64,512]{1,0:T(8,128)S(1)} collective-permute-done((f32[64,512]{1,0:T(8,128)S(1)}, f32[64,512]{1,0:T(8,128)S(1)}, u32[]{:S(2)}, u32[]{:S(2)}) %collective-permute-start.35) | collective-permute-done | bytes 131104 | tf_op jit(solution)/shard_map/ppermute | solution.py:234
  133.2 2.3 %collective-permute-done.37 = f32[64,512]{1,0:T(8,128)S(1)} collective-permute-done((f32[64,512]{1,0:T(8,128)S(1)}, f32[64,512]{1,0:T(8,128)S(1)}, u32[]{:S(2)}, u32[]{:S(2)}) %collective-permute-start.37) | collective-permute-done | bytes 131104 | tf_op jit(solution)/shard_map/ppermute | solution.py:234
  (83 shorter events, 26.4 us)
Async XLA Ops:
  0.6 7.4 %collective-permute-start.3 = (f32[64,512]{1,0:T(8,128)}, f32[64,512]{1,0:T(8,128)S(1)}, u32[]{:S(2)}, u32[]{:S(2)}) collective-permute-start(f32[64,512]{1,0:T(8,128)} %refs_0_.1), channel_id=1, source_target_pairs={{0,128},{32,160},{64,192},{96,224},{128,0},{160,32},{192,64},{224,... | collective-permute-start | bytes 393224 | tf_op jit(solution)/shard_map/ppermute | solution.py:234
  5.0 8.8 %collective-permute-start = (f32[64,512]{1,0:T(8,128)}, f32[64,512]{1,0:T(8,128)S(1)}, u32[]{:S(2)}, u32[]{:S(2)}) collective-permute-start(f32[64,512]{1,0:T(8,128)} %refs_0_.1), channel_id=1, source_target_pairs={{0,32},{32,0},{64,96},{96,64},{128,160},{160,128},{192,224},{224,1... | collective-permute-start | bytes 393224 | tf_op jit(solution)/shard_map/ppermute | solution.py:245
  5.0 7.3 %collective-permute-start.5 = (f32[64,512]{1,0:T(8,128)}, f32[64,512]{1,0:T(8,128)S(1)}, u32[]{:S(2)}, u32[]{:S(2)}) collective-permute-start(f32[64,512]{1,0:T(8,128)} %refs_0_.1), channel_id=1, source_target_pairs={{0,64},{32,96},{64,128},{96,160},{128,192},{160,224},{192,0},{224,... | collective-permute-start | bytes 393224 | tf_op jit(solution)/shard_map/ppermute | solution.py:234
  20.4 10.3 %collective-permute-start.7 = (f32[8,64,128]{2,1,0:T(8,128)S(1)}, f32[8,64,128]{2,1,0:T(8,128)S(1)}, u32[]{:S(2)}, u32[]{:S(2)}) collective-permute-start(f32[8,64,128]{2,1,0:T(8,128)S(1)} %get-tuple-element.36), channel_id=1, source_target_pairs={{0,8},{4,12},{8,16},{12,20},{16,24},{20,28},{24,0},{28,4},{1,9},{5... | collective-permute-start | bytes 786440 | tf_op jit(solution)/shard_map/ppermute | solution.py:234
  23.1 12.0 %collective-permute-start.8 = (f32[8,64,128]{2,1,0:T(8,128)S(1)}, f32[8,64,128]{2,1,0:T(8,128)S(1)}, u32[]{:S(2)}, u32[]{:S(2)}) collective-permute-start(f32[8,64,128]{2,1,0:T(8,128)S(1)} %get-tuple-element.37), channel_id=1, source_target_pairs={{0,16},{4,20},{8,24},{12,28},{16,0},{20,4},{24,8},{28,12},{1,17},{... | collective-permute-start | bytes 786440 | tf_op jit(solution)/shard_map/ppermute | solution.py:234
  25.4 12.4 %collective-permute-start.9 = (f32[8,64,128]{2,1,0:T(8,128)S(1)}, f32[8,64,128]{2,1,0:T(8,128)S(1)}, u32[]{:S(2)}, u32[]{:S(2)}) collective-permute-start(f32[8,64,128]{2,1,0:T(8,128)S(1)} %get-tuple-element.38), channel_id=1, source_target_pairs={{0,24},{4,28},{8,0},{12,4},{16,8},{20,12},{24,16},{28,20},{1,25},{... | collective-permute-start | bytes 786440 | tf_op jit(solution)/shard_map/ppermute | solution.py:234
  25.4 17.8 %collective-permute-start.17 = (f32[64,128]{1,0:T(8,128)S(1)}, f32[64,128]{1,0:T(8,128)S(1)}, u32[]{:S(2)}, u32[]{:S(2)}) collective-permute-start(f32[64,128]{1,0:T(8,128)S(1)} %get-tuple-element.48), channel_id=1, source_target_pairs={{0,1},{1,2},{2,3},{3,0},{4,5},{5,6},{6,7},{7,4},{8,9},{9,10},{10,1... | collective-permute-start | bytes 98312 | tf_op jit(solution)/shard_map/ppermute | solution.py:234
  27.4 19.5 %collective-permute-start.18 = (f32[64,128]{1,0:T(8,128)S(1)}, f32[64,128]{1,0:T(8,128)S(1)}, u32[]{:S(2)}, u32[]{:S(2)}) collective-permute-start(f32[64,128]{1,0:T(8,128)S(1)} %get-tuple-element.49), channel_id=1, source_target_pairs={{0,2},{1,3},{2,0},{3,1},{4,6},{5,7},{6,4},{7,5},{8,10},{9,11},{10,... | collective-permute-start | bytes 98312 | tf_op jit(solution)/shard_map/ppermute | solution.py:234
  30.7 17.1 %collective-permute-start.19 = (f32[64,128]{1,0:T(8,128)S(1)}, f32[64,128]{1,0:T(8,128)S(1)}, u32[]{:S(2)}, u32[]{:S(2)}) collective-permute-start(f32[64,128]{1,0:T(8,128)S(1)} %get-tuple-element.50), channel_id=1, source_target_pairs={{0,3},{1,0},{2,1},{3,2},{4,7},{5,4},{6,5},{7,6},{8,11},{9,8},{10,9... | collective-permute-start | bytes 98312 | tf_op jit(solution)/shard_map/ppermute | solution.py:234
  37.9 14.5 %collective-permute-start.10 = (f32[64,128]{1,0:T(8,128)S(1)}, f32[64,128]{1,0:T(8,128)S(1)}, u32[]{:S(2)}, u32[]{:S(2)}) collective-permute-start(f32[64,128]{1,0:T(8,128)S(1)} %get-tuple-element.40), channel_id=1, source_target_pairs={{0,1},{1,2},{2,3},{3,4},{4,5},{5,6},{6,7},{7,0},{8,9},{9,10},{10,1... | collective-permute-start | bytes 98312 | tf_op jit(solution)/shard_map/ppermute | solution.py:240
  39.9 15.2 %collective-permute-start.11 = (f32[64,128]{1,0:T(8,128)S(1)}, f32[64,128]{1,0:T(8,128)S(1)}, u32[]{:S(2)}, u32[]{:S(2)}) collective-permute-start(f32[64,128]{1,0:T(8,128)S(1)} %get-tuple-element.41), channel_id=1, source_target_pairs={{0,2},{1,3},{2,4},{3,5},{4,6},{5,7},{6,0},{7,1},{8,10},{9,11},{10,... | collective-permute-start | bytes 98312 | tf_op jit(solution)/shard_map/ppermute | solution.py:240
  43.2 13.0 %collective-permute-start.12 = (f32[64,128]{1,0:T(8,128)S(1)}, f32[64,128]{1,0:T(8,128)S(1)}, u32[]{:S(2)}, u32[]{:S(2)}) collective-permute-start(f32[64,128]{1,0:T(8,128)S(1)} %get-tuple-element.42), channel_id=1, source_target_pairs={{0,3},{1,4},{2,5},{3,6},{4,7},{5,0},{6,1},{7,2},{8,11},{9,12},{10,... | collective-permute-start | bytes 98312 | tf_op jit(solution)/shard_map/ppermute | solution.py:240
  46.9 9.3 %collective-permute-start.13 = (f32[64,128]{1,0:T(8,128)S(1)}, f32[64,128]{1,0:T(8,128)S(1)}, u32[]{:S(2)}, u32[]{:S(2)}) collective-permute-start(f32[64,128]{1,0:T(8,128)S(1)} %get-tuple-element.43), channel_id=1, source_target_pairs={{0,4},{1,5},{2,6},{3,7},{4,0},{5,1},{6,2},{7,3},{8,12},{9,13},{10,... | collective-permute-start | bytes 98312 | tf_op jit(solution)/shard_map/ppermute | solution.py:240
  47.7 8.5 %collective-permute-start.14 = (f32[64,128]{1,0:T(8,128)S(1)}, f32[64,128]{1,0:T(8,128)S(1)}, u32[]{:S(2)}, u32[]{:S(2)}) collective-permute-start(f32[64,128]{1,0:T(8,128)S(1)} %get-tuple-element.44), channel_id=1, source_target_pairs={{0,5},{1,6},{2,7},{3,0},{4,1},{5,2},{6,3},{7,4},{8,13},{9,14},{10,... | collective-permute-start | bytes 98312 | tf_op jit(solution)/shard_map/ppermute | solution.py:240
  59.8 9.5 %collective-permute-start.26 = (f32[3,64,128]{2,1,0:T(8,128)S(1)}, f32[3,64,128]{2,1,0:T(8,128)S(1)}, u32[]{:S(2)}, u32[]{:S(2)}) collective-permute-start(f32[3,64,128]{2,1,0:T(8,128)S(1)} %get-tuple-element.55.refs_0_), channel_id=1, source_target_pairs={{0,4},{1,5},{2,6},{3,7},{4,0},{5,1},{6,2},{7,3},{8,12},{9,13},{10,... | collective-permute-start | bytes 294920 | tf_op jit(solution)/shard_map/ppermute | solution.py:240
  61.4 15.3 %collective-permute-start.27 = (f32[3,64,128]{2,1,0:T(8,128)S(1)}, f32[3,64,128]{2,1,0:T(8,128)S(1)}, u32[]{:S(2)}, u32[]{:S(2)}) collective-permute-start(f32[3,64,128]{2,1,0:T(8,128)S(1)} %get-tuple-element.56), channel_id=1, source_target_pairs={{0,5},{1,6},{2,7},{3,0},{4,1},{5,2},{6,3},{7,4},{8,13},{9,14},{10,... | collective-permute-start | bytes 294920 | tf_op jit(solution)/shard_map/ppermute | solution.py:240
  64.2 14.3 %collective-permute-start.23 = (f32[3,64,128]{2,1,0:T(8,128)S(1)}, f32[3,64,128]{2,1,0:T(8,128)S(1)}, u32[]{:S(2)}, u32[]{:S(2)}) collective-permute-start(f32[3,64,128]{2,1,0:T(8,128)S(1)} %get-tuple-element.56), channel_id=1, source_target_pairs={{0,1},{1,2},{2,3},{3,4},{4,5},{5,6},{6,7},{7,0},{8,9},{9,10},{10,1... | collective-permute-start | bytes 294920 | tf_op jit(solution)/shard_map/ppermute | solution.py:240
  65.2 13.3 %collective-permute-start.28 = (f32[3,64,128]{2,1,0:T(8,128)S(1)}, f32[3,64,128]{2,1,0:T(8,128)S(1)}, u32[]{:S(2)}, u32[]{:S(2)}) collective-permute-start(f32[3,64,128]{2,1,0:T(8,128)S(1)} %get-tuple-element.57), channel_id=1, source_target_pairs={{0,6},{1,7},{2,0},{3,1},{4,2},{5,3},{6,4},{7,5},{8,14},{9,15},{10,... | collective-permute-start | bytes 294920 | tf_op jit(solution)/shard_map/ppermute | solution.py:240
  68.0 10.5 %collective-permute-start.24 = (f32[3,64,128]{2,1,0:T(8,128)S(1)}, f32[3,64,128]{2,1,0:T(8,128)S(1)}, u32[]{:S(2)}, u32[]{:S(2)}) collective-permute-start(f32[3,64,128]{2,1,0:T(8,128)S(1)} %get-tuple-element.57), channel_id=1, source_target_pairs={{0,2},{1,3},{2,4},{3,5},{4,6},{5,7},{6,0},{7,1},{8,10},{9,11},{10,... | collective-permute-start | bytes 294920 | tf_op jit(solution)/shard_map/ppermute | solution.py:240
  69.2 10.8 %collective-permute-start.29 = (f32[3,64,128]{2,1,0:T(8,128)S(1)}, f32[3,64,128]{2,1,0:T(8,128)S(1)}, u32[]{:S(2)}, u32[]{:S(2)}) collective-permute-start(f32[3,64,128]{2,1,0:T(8,128)S(1)} %get-tuple-element.58), channel_id=1, source_target_pairs={{0,7},{1,0},{2,1},{3,2},{4,3},{5,4},{6,5},{7,6},{8,15},{9,8},{10,9... | collective-permute-start | bytes 294920 | tf_op jit(solution)/shard_map/ppermute | solution.py:240
  76.7 7.7 %collective-permute-start.25 = (f32[3,64,128]{2,1,0:T(8,128)S(1)}, f32[3,64,128]{2,1,0:T(8,128)S(1)}, u32[]{:S(2)}, u32[]{:S(2)}) collective-permute-start(f32[3,64,128]{2,1,0:T(8,128)S(1)} %get-tuple-element.58), channel_id=1, source_target_pairs={{0,3},{1,4},{2,5},{3,6},{4,7},{5,0},{6,1},{7,2},{8,11},{9,12},{10,... | collective-permute-start | bytes 294920 | tf_op jit(solution)/shard_map/ppermute | solution.py:240
  84.5 10.8 %collective-permute-start.32 = (f32[10,64,128]{2,1,0:T(8,128)S(1)}, f32[10,64,128]{2,1,0:T(8,128)S(1)}, u32[]{:S(2)}, u32[]{:S(2)}) collective-permute-start(f32[10,64,128]{2,1,0:T(8,128)S(1)} %shard_map.107.refs_0_), channel_id=1, source_target_pairs={{0,8},{4,12},{8,16},{12,20},{16,24},{20,28},{24,0},{28,4},{1,9},{5... | collective-permute-start | bytes 983048 | tf_op jit(solution)/shard_map/ppermute | solution.py:234
  85.3 12.7 %collective-permute-start.31 = (f32[10,64,128]{2,1,0:T(8,128)S(1)}, f32[10,64,128]{2,1,0:T(8,128)S(1)}, u32[]{:S(2)}, u32[]{:S(2)}) collective-permute-start(f32[10,64,128]{2,1,0:T(8,128)S(1)} %shard_map.107.refs_0_), channel_id=1, source_target_pairs={{0,16},{4,20},{8,24},{12,28},{16,0},{20,4},{24,8},{28,12},{1,17},{... | collective-permute-start | bytes 983048 | tf_op jit(solution)/shard_map/ppermute | solution.py:234
  89.5 12.2 %collective-permute-start.30 = (f32[10,64,128]{2,1,0:T(8,128)S(1)}, f32[10,64,128]{2,1,0:T(8,128)S(1)}, u32[]{:S(2)}, u32[]{:S(2)}) collective-permute-start(f32[10,64,128]{2,1,0:T(8,128)S(1)} %shard_map.107.refs_0_), channel_id=1, source_target_pairs={{0,24},{4,28},{8,0},{12,4},{16,8},{20,12},{24,16},{28,20},{1,25},{... | collective-permute-start | bytes 983048 | tf_op jit(solution)/shard_map/ppermute | solution.py:234
  108.8 16.3 %collective-permute-start.34 = (f32[64,512]{1,0:T(8,128)S(1)}, f32[64,512]{1,0:T(8,128)S(1)}, u32[]{:S(2)}, u32[]{:S(2)}) collective-permute-start(f32[64,512]{1,0:T(8,128)S(1)} %get-tuple-element.62), channel_id=1, source_target_pairs={{0,32},{32,0},{64,96},{96,64},{128,160},{160,128},{192,224},{224,1... | collective-permute-start | bytes 393224 | tf_op jit(solution)/shard_map/ppermute | solution.py:245
  108.9 17.0 %collective-permute-start.36 = (f32[64,512]{1,0:T(8,128)S(1)}, f32[64,512]{1,0:T(8,128)S(1)}, u32[]{:S(2)}, u32[]{:S(2)}) collective-permute-start(f32[64,512]{1,0:T(8,128)S(1)} %get-tuple-element.64), channel_id=1, source_target_pairs={{0,32},{32,0},{64,96},{96,64},{128,160},{160,128},{192,224},{224,1... | collective-permute-start | bytes 393224 | tf_op jit(solution)/shard_map/ppermute | solution.py:245
  109.4 18.6 %collective-permute-start.38 = (f32[64,512]{1,0:T(8,128)S(1)}, f32[64,512]{1,0:T(8,128)S(1)}, u32[]{:S(2)}, u32[]{:S(2)}) collective-permute-start(f32[64,512]{1,0:T(8,128)S(1)} %get-tuple-element.66), channel_id=1, source_target_pairs={{0,32},{32,0},{64,96},{96,64},{128,160},{160,128},{192,224},{224,1... | collective-permute-start | bytes 393224 | tf_op jit(solution)/shard_map/ppermute | solution.py:245
  109.6 11.1 %collective-permute-start.21 = (f32[64,128]{1,0:T(8,128)S(1)}, f32[64,128]{1,0:T(8,128)S(1)}, u32[]{:S(2)}, u32[]{:S(2)}) collective-permute-start(f32[64,128]{1,0:T(8,128)S(1)} %get-tuple-element.53), channel_id=1, source_target_pairs={{0,2},{1,3},{2,0},{3,1},{4,6},{5,7},{6,4},{7,5},{8,10},{9,11},{10,... | collective-permute-start | bytes 98312 | tf_op jit(solution)/shard_map/ppermute | solution.py:234
  115.6 13.8 %collective-permute-start.42 = (f32[2,64,128]{2,1,0:T(8,128)S(1)}, f32[2,64,128]{2,1,0:T(8,128)S(1)}, u32[]{:S(2)}, u32[]{:S(2)}) collective-permute-start(f32[2,64,128]{2,1,0:T(8,128)S(1)} %add.63), channel_id=1, source_target_pairs={{0,128},{32,160},{64,192},{96,224},{128,0},{160,32},{192,64},{224,... | collective-permute-start | bytes 196616 | tf_op jit(solution)/shard_map/ppermute | solution.py:245
  125.2 8.0 %collective-permute-start.35 = (f32[64,512]{1,0:T(8,128)S(1)}, f32[64,512]{1,0:T(8,128)S(1)}, u32[]{:S(2)}, u32[]{:S(2)}) collective-permute-start(f32[64,512]{1,0:T(8,128)S(1)} %add.56), channel_id=1, source_target_pairs={{0,128},{32,160},{64,192},{96,224},{128,0},{160,32},{192,64},{224,... | collective-permute-start | bytes 393224 | tf_op jit(solution)/shard_map/ppermute | solution.py:234
  125.9 9.6 %collective-permute-start.37 = (f32[64,512]{1,0:T(8,128)S(1)}, f32[64,512]{1,0:T(8,128)S(1)}, u32[]{:S(2)}, u32[]{:S(2)}) collective-permute-start(f32[64,512]{1,0:T(8,128)S(1)} %add.58), channel_id=1, source_target_pairs={{0,64},{32,96},{64,128},{96,160},{128,192},{160,224},{192,0},{224,... | collective-permute-start | bytes 393224 | tf_op jit(solution)/shard_map/ppermute | solution.py:234
  128.1 7.4 %collective-permute-start.39 = (f32[64,512]{1,0:T(8,128)S(1)}, f32[64,512]{1,0:T(8,128)S(1)}, u32[]{:S(2)}, u32[]{:S(2)}) collective-permute-start(f32[64,512]{1,0:T(8,128)S(1)} %add.60), channel_id=1, source_target_pairs={{0,192},{32,224},{64,0},{96,32},{128,64},{160,96},{192,128},{224,1... | collective-permute-start | bytes 393224 | tf_op jit(solution)/shard_map/ppermute | solution.py:234
  (14 other events, 115.7 us)
